TPU v7x, 32 devices: a whole 2x2x4 slice. The times are simulated.
32 devices in a mesh: dp: 2 (over x), ctx: 8 (over z, y), head: 2 (over core).
Axes of the slice: x: 2, y: 2, z: 4, core: 2. Of those that a mesh axis runs over, the one named last changes fastest.
Arguments:
- queries: bfloat16 [2, 1024, 4096], P('dp', 'ctx', 'head'), may hold values from -200 to 200
- targets: bfloat16 [2, 1024, 4096], P('dp', 'ctx', 'head'), may hold values from -3 to 3
- document_keys: bfloat16 [2, 1024, 256], P('dp', 'ctx', 'head'), may hold values from -6 to 6
- document_values: bfloat16 [2, 1024, 256], P('dp', 'ctx', 'head'), may hold values from -6 to 6
- doc_pos: int32 [2, 1024], P('dp', 'ctx'), may hold values from 0 to 1023, each once within a row
- cart_keys: bfloat16 [128, 256], P('ctx', 'head'), may hold values from -8 to 8
- cartridge_values: bfloat16 [128, 256], P('ctx', 'head'), may hold values from -6 to 6
- master: float32 [128, 2, 256], P('ctx', 'head', 'dp'), may hold values from -5 to 5
- first_moment1: float32 [128, 2, 256], P('ctx', 'head', 'dp'), may hold values from -4 to 4
- second_moment2: float32 [128, 2, 256], P('ctx', 'head', 'dp'), may hold values from 0.1 to 2
Outputs:
- new_out: bfloat16 [2, 1024, 4096], P('dp', 'ctx', 'head')
- new_master: float32 [128, 2, 256], P('ctx', 'head', 'dp')
- new_moment1: float32 [128, 2, 256], P('ctx', 'head', 'dp')
- new_moment2: float32 [128, 2, 256], P('ctx', 'head', 'dp')
Inputs may be any that keep to these rules, and one draw needn't show every extreme that they name: Each row of doc_pos holds every position of the document once.
All inputs are finite; a program needn't handle non-finite values.
Results may differ from a plain program's by a relative error of at most 0.015.
Values may be sent and summed in bfloat16 or wider, within the bound.
No kernel may reach another device: no remote copies, remote signals or barrier semaphores. Data moves between devices by JAX's collectives and lax.ppermute only.
A program may use at most 64 MiB of HBM per device.

v0:
```python
import functools
import math

import jax
import jax.numpy as jnp
from jax import lax
from jax.experimental import pallas as pl
from jax.experimental.pallas import tpu as pltpu
from jax.sharding import PartitionSpec as P


beta_one = 0.8
beta_two = 0.95
learn_rate = 0.1
adam_eps = 1e-08
norm_eps = 1e-06
neg_big = -1e30
log2_e = math.log2(math.e)
pos_base = 256.0
f32, bf16 = jnp.float32, jnp.bfloat16


def xor_steps(size):
    assert size & (size - 1) == 0
    return [1 << b for b in reversed(range(size.bit_length() - 1))]


def swap(x, axis, mask, size):
    return lax.ppermute(x, axis, [(i, i ^ mask) for i in range(size)])


def place(mask, steps):
    at = 0
    for n, step in enumerate(steps):
        bit = step.bit_length() - 1
        at = at + (((mask >> bit) & 1) << n)
    return at


def nt(a, b):
    return lax.dot_general(a, b, (((1,), (1,)), ((), ())), preferred_element_type=f32)


def tn(a, b):
    return lax.dot_general(a, b, (((0,), (0,)), ((), ())), preferred_element_type=f32)


def nn(a, b):
    return jnp.dot(a, b, preferred_element_type=f32)


def pack_kernel(k, v, pos, ck, cv, ma, m1, m2, msg, st, line, sems):
    rows, crows, hd = k.shape[1], ck.shape[0], k.shape[2]
    at = 2 * rows
    copies = [
        (k.at[0], msg.at[0:rows]),
        (v.at[0], msg.at[rows:at]),
        (ck, msg.at[at : at + crows]),
        (cv, msg.at[at + crows : at + 2 * crows]),
        (pos, line),
    ]
    copies += [(ref.at[:, 0, :], st.at[n * crows : (n + 1) * crows]) for n, ref in enumerate((ma, m1, m2))]
    started = [pltpu.make_async_copy(x, y, sems.at[n]) for n, (x, y) in enumerate(copies)]
    for copy in started:
        copy.start()
    for copy in started:
        copy.wait()
    at += 2 * crows
    p = line[...].astype(f32)
    hi = jnp.floor(p * (1.0 / pos_base))
    lo = p - hi * pos_base
    row = lax.broadcasted_iota(jnp.int32, (16, hd), 0)
    both = jnp.where(row == 0, jnp.broadcast_to(hi, (16, hd)), jnp.broadcast_to(lo, (16, hd)))
    msg[at : at + 16] = both.astype(bf16)


def split(refs, stride):
    return [(ref, j * stride) for ref in refs for j in range(ref.shape[0] // stride)]


def positions(ref, at, stride):
    two_rows = ref[at + stride - 16 : at + stride].astype(f32)
    return two_rows[0:1] * pos_base + two_rows[1:2]


def document_part(own, blocks, rows, stride):
    query_pos = jnp.broadcast_to(positions(own, 0, stride), (rows, rows))
    keys, values = [], []
    for ref, at in blocks:
        key_pos = jnp.broadcast_to(positions(ref, at, stride), (rows, rows)).T
        barred = jnp.where(key_pos <= query_pos, 0.0, neg_big).astype(bf16)
        keys.append(jnp.concatenate([ref[at : at + rows], barred], axis=1))
        values.append(ref[at + rows : at + 2 * rows])
    values = jnp.concatenate(values, axis=0)
    return jnp.concatenate(keys, axis=0), jnp.concatenate([values, jnp.ones_like(values)], axis=1)


def heads_of(ref, b, per, hd):
    return jnp.concatenate([ref[:, h * hd : (h + 1) * hd] for h in range(b * per, (b + 1) * per)], axis=0)


def pick(rows, per):
    line = lax.broadcasted_iota(jnp.int32, (rows, rows), 0)
    lane = lax.broadcasted_iota(jnp.int32, (rows, rows), 1)
    one = jnp.where(line == lane, 1.0, 0.0).astype(bf16)
    return jnp.concatenate([one] * per, axis=0)


def wide(x, columns):
    return jnp.concatenate([x] * (columns // x.shape[1]), axis=1)


def attend(qx, part, two, state):
    keys, values = part
    s = nt(qx, keys) * two
    top = jnp.max(s, axis=1, keepdims=True)
    hd = values.shape[1] // 2
    if state is None:
        top = jnp.broadcast_to(top, (s.shape[0], hd))
        both = nn(jnp.exp2(s - wide(top, s.shape[1])).astype(bf16), values)
        return both[:, :hd], both[:, hd:], top
    acc, total, old = state
    top = jnp.maximum(old, top)
    both = nn(jnp.exp2(s - wide(top, s.shape[1])).astype(bf16), values)
    keep = jnp.exp2(old - top)
    return acc * keep + both[:, :hd], total * keep + both[:, hd:], top


def chunk_kernel(n_msgs, scale, per, rows, stride, *refs):
    q, own, msgs = refs[0], refs[1], refs[2 : 2 + n_msgs]
    outs = refs[2 + n_msgs :]
    hd = own.shape[1]
    part = document_part(own, split(msgs, stride), rows, stride)
    eye = pick(rows, per)
    span = per * rows
    for b in range(q.shape[1] // hd // per):
        cut = slice(b * span, (b + 1) * span)
        qx = jnp.concatenate([heads_of(q, b, per, hd), eye], axis=1)
        for ref, x in zip(outs, attend(qx, part, scale * log2_e, None)):
            ref[cut] = x


def gradient_kernel(n_last, masks, scale, per, rows, stride, *refs):
    q, t = refs[:2]
    olds = refs[2:5]
    outs, grad = refs[-4:-1], refs[-1]
    msgs = refs[5:-4]
    own = msgs[0]
    hd = own.shape[1]
    crows = (stride - 2 * rows - 16) // 2
    me = lax.axis_index("ctx")
    two = scale * log2_e
    part = document_part(own, split(msgs[len(msgs) - n_last :], stride), rows, stride)
    every = [(ref, at + 2 * rows) for ref, at in split(msgs, stride)]
    cart_k = jnp.concatenate([ref[at : at + crows] for ref, at in every], axis=0)
    cart_v = jnp.concatenate([ref[at + crows : at + 2 * crows] for ref, at in every], axis=0)
    cart_vx = jnp.concatenate([cart_v, jnp.ones_like(cart_v)], axis=1)
    n_cart = cart_k.shape[0]
    eye = pick(rows, per)
    span = per * rows
    gk = jnp.zeros((n_cart, hd), f32)
    gv = jnp.zeros((n_cart, hd), f32)
    for b in range(q.shape[1] // hd // per):
        cut = slice(b * span, (b + 1) * span)
        qh = heads_of(q, b, per, hd)
        acc, total, top = attend(jnp.concatenate([qh, eye], axis=1), part, two, tuple(ref[cut] for ref in olds))
        for ref, x in zip(outs, (acc, total, top)):
            ref[cut] = x
        sc = nt(qh, cart_k) * two
        both = jnp.maximum(top, jnp.max(sc, axis=1, keepdims=True))
        wc = jnp.exp2(sc - wide(both, n_cart))
        keep = jnp.exp2(top - both)
        more = nn(wc.astype(bf16), cart_vx)
        inv = 1.0 / (total * keep + more[:, hd:])
        out = (acc * keep + more[:, :hd]) * inv
        d_out = out - heads_of(t, b, per, hd).astype(f32)
        delta = jnp.sum(d_out * out, axis=1, keepdims=True)
        d_out_b = d_out.astype(bf16)
        probs = wc * wide(inv, n_cart)
        ds = probs * (nt(d_out_b, cart_v) - delta)
        gk = gk + tn(ds.astype(bf16), qh)
        gv = gv + tn(probs.astype(bf16), d_out_b)
    whole = jnp.concatenate([gk * scale, gv], axis=1).astype(bf16)
    for j, mask in enumerate(masks):
        to = pl.multiple_of((me ^ mask) * crows, crows)
        grad[pl.ds(to, crows)] = whole[j * crows : (j + 1) * crows]


def square_kernel(a, b, total, squares):
    g = a[...].astype(f32) + b[...].astype(f32)
    total[...] = g
    squares[...] = jnp.broadcast_to(jnp.sum(g * g, keepdims=True), squares.shape)


def update(g, ma, m1, m2):
    one = beta_one * m1 + (1.0 - beta_one) * g
    two = beta_two * m2 + (1.0 - beta_two) * g * g
    return one, two, ma - learn_rate * one / (jnp.sqrt(two) + adam_eps)


def final_kernel(masks, dp_steps, scale, per, count, q, acc_in, total_in, top_in, g, sq_a, sq_b, st, ma, m1, m2, out, ma_o, m1_o, m2_o, cart):
    rows, hd = q.shape[0], acc_in.shape[1]
    group = q.shape[1] // hd
    n_dp = 1 << len(dp_steps)
    crows, width = ma.shape[0], ma.shape[2]
    me, my_dp = lax.axis_index("ctx"), lax.axis_index("dp")
    two = scale * log2_e
    mean = (sq_a[0:1, 0:1] + sq_b[0:1, 0:1]) * (1.0 / count)
    inv_rms = 1.0 / jnp.sqrt(mean + norm_eps)
    mine = g[pl.ds(pl.multiple_of(me * crows, crows), crows)]
    own = mine[:, 0:width]
    for d in range(1, n_dp):
        own = jnp.where(my_dp == d, mine[:, d * width : (d + 1) * width], own)
    one, sec, new = update(own * inv_rms, ma[:, 0, :], m1[:, 0, :], m2[:, 0, :])
    m1_o[:, 0, :] = one
    m2_o[:, 0, :] = sec
    ma_o[:, 0, :] = new
    for r, mask in enumerate(masks):
        parts = [[], [], []]
        for d in range(n_dp):
            at = (r * n_dp + place(my_dp ^ d, dp_steps)) * 3 * crows
            for n in range(3):
                parts[n].append(st[pl.ds(pl.multiple_of(at + n * crows, crows), crows)])
        ma_r, m1_r, m2_r = (jnp.concatenate(x, axis=1) for x in parts)
        rows_g = g[pl.ds(pl.multiple_of((me ^ mask) * crows, crows), crows)]
        _, _, new = update(rows_g * inv_rms, ma_r, m1_r, m2_r)
        cart[r * crows : (r + 1) * crows] = new.astype(bf16)
    cart_k = cart[:, :hd]
    cart_v = cart[:, hd:]
    cart_vx = jnp.concatenate([cart_v, jnp.ones_like(cart_v)], axis=1)
    span = per * rows
    for b in range(group // per):
        heads = range(b * per, (b + 1) * per)
        qh = jnp.concatenate([q[:, h * hd : (h + 1) * hd] for h in heads], axis=0)
        cut = slice(b * span, (b + 1) * span)
        top = top_in[cut]
        sc = nt(qh, cart_k) * two
        both = jnp.maximum(top, jnp.max(sc, axis=1, keepdims=True))
        wc = jnp.exp2(sc - wide(both, sc.shape[1])).astype(bf16)
        keep = jnp.exp2(top - both)
        more = nn(wc, cart_vx)
        res = ((acc_in[cut] * keep + more[:, :hd]) / (total_in[cut] * keep + more[:, hd:])).astype(bf16)
        for n, h in enumerate(heads):
            out[:, h * hd : (h + 1) * hd] = res[n * rows : (n + 1) * rows]


VMEM = pl.BlockSpec(memory_space=pltpu.VMEM)


def call(body, outs, n_in, scratch=(), limit=40):
    return pl.pallas_call(
        body,
        out_shape=outs,
        in_specs=[VMEM] * n_in,
        out_specs=tuple(VMEM for _ in outs),
        scratch_shapes=list(scratch),
        compiler_params=pltpu.CompilerParams(vmem_limit_bytes=limit * 2**20),
    )


def local(sizes, queries, targets, document_keys, document_values, doc_pos, cart_keys, cartridge_values, master, first_moment1, second_moment2):
    n_dp, n_ctx, n_head = sizes
    hd = document_keys.shape[2]
    rows = queries.shape[1]
    group = queries.shape[2] // hd
    crows = cart_keys.shape[0]
    scale = hd ** (-0.5)
    per = math.gcd(group, 4)
    steps, dp_steps, head_steps = xor_steps(n_ctx), xor_steps(n_dp), xor_steps(n_head)
    sds = jax.ShapeDtypeStruct
    stride = 2 * rows + 2 * crows + 16
    masks = [0]
    for s in steps:
        masks += [m ^ s for m in masks]
    msg, st = pl.pallas_call(
        pack_kernel,
        out_shape=(sds((stride, hd), bf16), sds((3 * crows, master.shape[2]), f32)),
        in_specs=[pl.BlockSpec(memory_space=pltpu.HBM)] * 8,
        out_specs=(VMEM, VMEM),
        scratch_shapes=[pltpu.VMEM(doc_pos.shape, jnp.int32), pltpu.SemaphoreType.DMA((8,))],
        compiler_params=pltpu.CompilerParams(vmem_limit_bytes=8 * 2**20),
    )(
        *(
            pltpu.with_memory_space_constraint(x, pltpu.HBM)
            for x in (document_keys, document_values, doc_pos, cart_keys, cartridge_values, master, first_moment1, second_moment2)
        )
    )
    q, t = queries[0], targets[0]
    cart = n_ctx * crows
    shapes = (sds((rows * group, hd), f32),) * 3
    last = steps[-1]
    pieces, mirrored, held = [msg], [], msg
    for s in steps[:-1]:
        piece = swap(held, "ctx", s, n_ctx)
        mirrored.append(swap(pieces[-1], "ctx", last, n_ctx))
        held = jnp.concatenate([held, piece], axis=0)
        pieces.append(piece)
    mirrored.append(swap(pieces[-1], "ctx", last, n_ctx))
    msgs = pieces + mirrored
    body = functools.partial(chunk_kernel, len(msgs) - 1, scale, per, rows, stride)
    state = call(body, shapes, 1 + len(msgs))(q, msg, *msgs[:-1])
    for axis, s, size in [("dp", s, n_dp) for s in dp_steps] + [("ctx", s, n_ctx) for s in steps]:
        more = swap(st, axis, s, size)
        st = jnp.concatenate([st, more], axis=0)
    body = functools.partial(gradient_kernel, 1, masks, scale, math.gcd(group, 8), rows, stride)
    *state, grad = call(body, shapes + (sds((cart, 2 * hd), bf16),), 5 + len(msgs))(q, t, *state, *msgs)
    chain = [("dp", s, n_dp) for s in dp_steps] + [("ctx", s, n_ctx) for s in steps]
    for n, (axis, s, size) in enumerate(chain):
        other = swap(grad, axis, s, size)
        if n + 1 < len(chain):
            grad = (grad.astype(f32) + other.astype(f32)).astype(bf16)
    total, squares = call(square_kernel, (sds((cart, 2 * hd), f32), sds((8, hd), f32)), 2)(grad, other)
    mine = squares
    theirs = jnp.zeros_like(squares)
    for n, s in enumerate(head_steps):
        if n:
            mine = mine + theirs
        theirs = swap(mine, "head", s, n_head)
    count = master.size * n_dp * n_ctx * n_head
    new_out, new_master, new_m1, new_m2 = call(
        functools.partial(final_kernel, masks, dp_steps, scale, per, count),
        (sds((rows, group * hd), bf16), sds(master.shape, f32), sds(master.shape, f32), sds(master.shape, f32)),
        11,
        [pltpu.VMEM((cart, 2 * hd), bf16)],
    )(q, *state, total, mine, theirs, st, master, first_moment1, second_moment2)
    return (new_out[None], new_master, new_m1, new_m2)


def solution(mesh):
    in_specs = (
        P("dp", "ctx", "head"),
        P("dp", "ctx", "head"),
        P("dp", "ctx", "head"),
        P("dp", "ctx", "head"),
        P("dp", "ctx"),
        P("ctx", "head"),
        P("ctx", "head"),
        P("ctx", "head", "dp"),
        P("ctx", "head", "dp"),
        P("ctx", "head", "dp"),
    )
    out_specs = (
        P("dp", "ctx", "head"),
        P("ctx", "head", "dp"),
        P("ctx", "head", "dp"),
        P("ctx", "head", "dp"),
    )
    sizes = (mesh.shape["dp"], mesh.shape["ctx"], mesh.shape["head"])

    def step(*args):
        return local(sizes, *args)

    return jax.shard_map(step, mesh=mesh, in_specs=in_specs, out_specs=out_specs, check_vma=False)
```

profile of v0, /device:TPU:0, one launch (start us, length us, event | category | flops | bytes accessed | tf_op | source)
XLA Modules:
  0.0 51.2 jit_solution(6825192852144107066)
XLA Ops:
  0.6 0.0 copy-start
  0.6 0.9 %shard_map.129 = (bf16[304,128]{1,0:T(8,128)(2,1)S(1)}, f32[48,128]{1,0:T(8,128)S(1)}) custom-call(bf16[1,128,128]{2,1,0:T(8,128)(2,1)} %k.1, bf16[1,128,128]{2,1,0:T(8,128)(2,1)} %v.1, s32[1,128]{1,0:T(1,128)} %pos.1, bf16[16,128]{1,0:T(8,128)(2,1)} %ck.1, bf16[16,128]{1,0:T(8,128)(2,1)} %cv.1, f32[16,1,128]{2,1,0:T(1,128)} %ma.3, f32[16,1,128]{2,1,0:T(1,128)} %m1.3, ...), custom_call_target="tpu_custom_call" | custom-call | tf_op jit(solution)/shard_map/pallas_call | solution.py:275
  1.6 4.1 %collective-permute-start = (bf16[304,128]{1,0:T(8,128)(2,1)S(1)}, bf16[304,128]{1,0:T(8,128)(2,1)S(1)}, u32[]{:S(2)}, u32[]{:S(2)}) collective-permute-start(bf16[304,128]{1,0:T(8,128)(2,1)S(1)} %get-tuple-element.19.refs_1_.refs_2_.refs_5_), channel_id=1, source_target_pairs={{0,8},{2,10},{4,12},{6,14},{8,0},{10,2},{12,4},{14,6},{1,9},{3,11}... | collective-permute-start | bytes 233480 | tf_op jit(solution)/shard_map/ppermute | solution.py:29
  5.7 4.0 %collective-permute-done.refs_3_.refs_6_ = bf16[304,128]{1,0:T(8,128)(2,1)S(1)} collective-permute-done((bf16[304,128]{1,0:T(8,128)(2,1)S(1)}, bf16[304,128]{1,0:T(8,128)(2,1)S(1)}, u32[]{:S(2)}, u32[]{:S(2)}) %collective-permute-start) | collective-permute-done | bytes 77856 | tf_op jit(solution)/shard_map/ppermute | solution.py:29
  9.8 0.8 %collective-permute-start.1 = (bf16[608,128]{1,0:T(8,128)(2,1)S(1)}, bf16[608,128]{1,0:T(8,128)(2,1)S(1)}, u32[]{:S(2)}, u32[]{:S(2)}) collective-permute-start(bf16[608,128]{1,0:T(8,128)(2,1)S(1)} %pad_maximum_fusion.1), channel_id=1, source_target_pairs={{0,4},{2,6},{4,0},{6,2},{8,12},{10,14},{12,8},{14,10},{1,5},{3,7},... | collective-permute-start | bytes 466952 | tf_op jit(solution)/shard_map/ppermute | solution.py:29
  10.6 1.5 %collective-permute-start.2 = (bf16[304,128]{1,0:T(8,128)(2,1)S(1)}, bf16[304,128]{1,0:T(8,128)(2,1)S(1)}, u32[]{:S(2)}, u32[]{:S(2)}) collective-permute-start(bf16[304,128]{1,0:T(8,128)(2,1)S(1)} %get-tuple-element.19.refs_1_.refs_2_.refs_5_), channel_id=1, source_target_pairs={{0,2},{2,0},{4,6},{6,4},{8,10},{10,8},{12,14},{14,12},{1,3},{3,1},... | collective-permute-start | bytes 233480 | tf_op jit(solution)/shard_map/ppermute | solution.py:29
  12.1 1.5 %collective-permute-start.10 = (f32[48,128]{1,0:T(8,128)S(1)}, f32[48,128]{1,0:T(8,128)S(1)}, u32[]{:S(2)}, u32[]{:S(2)}) collective-permute-start(f32[48,128]{1,0:T(8,128)S(1)} %get-tuple-element.29), channel_id=1, source_target_pairs={{0,16},{16,0},{1,17},{17,1},{2,18},{18,2},{3,19},{19,3},{4,20},{20... | collective-permute-start | bytes 73736 | tf_op jit(solution)/shard_map/ppermute | solution.py:29
  13.6 1.5 %collective-permute-done.1.refs_4_.refs_7_ = bf16[608,128]{1,0:T(8,128)(2,1)S(1)} collective-permute-done((bf16[608,128]{1,0:T(8,128)(2,1)S(1)}, bf16[608,128]{1,0:T(8,128)(2,1)S(1)}, u32[]{:S(2)}, u32[]{:S(2)}) %collective-permute-start.1) | collective-permute-done | bytes 155680 | tf_op jit(solution)/shard_map/ppermute | solution.py:29
  15.1 1.7 %collective-permute-start.4 = (bf16[608,128]{1,0:T(8,128)(2,1)S(1)}, bf16[608,128]{1,0:T(8,128)(2,1)S(1)}, u32[]{:S(2)}, u32[]{:S(2)}) collective-permute-start(bf16[608,128]{1,0:T(8,128)(2,1)S(1)} %collective-permute-done.1.refs_4_.refs_7_), channel_id=1, source_target_pairs={{0,2},{2,0},{4,6},{6,4},{8,10},{10,8},{12,14},{14,12},{1,3},{3,1},... | collective-permute-start | bytes 466952 | tf_op jit(solution)/shard_map/ppermute | solution.py:29
  16.8 0.0 collective-permute-done.10
  16.8 2.7 %collective-permute-start.11 = (f32[96,128]{1,0:T(8,128)S(1)}, f32[96,128]{1,0:T(8,128)S(1)}, u32[]{:S(2)}, u32[]{:S(2)}) collective-permute-start(f32[96,128]{1,0:T(8,128)S(1)} %pad_maximum_fusion.3), channel_id=1, source_target_pairs={{0,8},{2,10},{4,12},{6,14},{8,0},{10,2},{12,4},{14,6},{1,9},{3,11}... | collective-permute-start | bytes 147464 | tf_op jit(solution)/shard_map/ppermute | solution.py:29
  19.5 0.5 collective-permute-start.3
  20.0 0.0 collective-permute-done.2.refs_5_.refs_8_
  20.0 3.9 %collective-permute-done.3.refs_6_.refs_9_ = bf16[304,128]{1,0:T(8,128)(2,1)S(1)} collective-permute-done((bf16[304,128]{1,0:T(8,128)(2,1)S(1)}, bf16[304,128]{1,0:T(8,128)(2,1)S(1)}, u32[]{:S(2)}, u32[]{:S(2)}) %collective-permute-start.3) | collective-permute-done | bytes 77856 | tf_op jit(solution)/shard_map/ppermute | solution.py:29
  23.9 0.0 copy-done
  23.9 0.0 copy-start.1
  23.9 2.6 %shard_map.130 = (f32[2048,128]{1,0:T(8,128)S(1)}, f32[2048,128]{1,0:T(8,128)S(1)}, f32[2048,128]{1,0:T(8,128)S(1)}) custom-call(bf16[128,2048]{1,0:T(8,128)(2,1)S(1)} %bitcast.3, bf16[304,128]{1,0:T(8,128)(2,1)S(1)} %get-tuple-element.19.refs_1_.refs_2_.refs_5_, bf16[304,128]{1,0:T(8,128)(2,1)S(1)} %get-tuple-element.19.refs_1_.refs_2_.refs_5_, ...), custom_call_target="tpu_custom_call" | custom-call | tf_op jit(solution)/shard_map/pallas_call | solution.py:301
  26.5 0.0 collective-permute-done.4.refs_10_
  26.5 0.0 copy-done.1
  26.5 2.9 %shard_map.131 = (f32[2048,128]{1,0:T(8,128)S(1)}, f32[2048,128]{1,0:T(8,128)S(1)}, f32[2048,128]{1,0:T(8,128)S(1)}, bf16[128,256]{1,0:T(8,128)(2,1)S(1)}) custom-call(bf16[128,2048]{1,0:T(8,128)(2,1)S(1)} %bitcast.4, bf16[128,2048]{1,0:T(8,128)(2,1)S(1)} %bitcast.6, f32[2048,128]{1,0:T(8,128)S(1)} %get-tuple-element.20.refs_2_, ...), custom_call_target="tpu_custom_call" | custom-call | tf_op jit(solution)/shard_map/pallas_call | solution.py:306
  29.4 1.6 %collective-permute-start.5 = (bf16[128,256]{1,0:T(8,128)(2,1)S(1)}, bf16[128,256]{1,0:T(8,128)(2,1)S(1)}, u32[]{:S(2)}, u32[]{:S(2)}) collective-permute-start(bf16[128,256]{1,0:T(8,128)(2,1)S(1)} %get-tuple-element.26), channel_id=1, source_target_pairs={{0,16},{16,0},{1,17},{17,1},{2,18},{18,2},{3,19},{19,3},{4,20},{20... | collective-permute-start | bytes 196616 | tf_op jit(solution)/shard_map/ppermute | solution.py:29
  30.9 0.0 collective-permute-done.11
  31.0 1.8 %collective-permute-start.12 = (f32[192,128]{1,0:T(8,128)S(1)}, f32[192,128]{1,0:T(8,128)S(1)}, u32[]{:S(2)}, u32[]{:S(2)}) collective-permute-start(f32[192,128]{1,0:T(8,128)S(1)} %pad_maximum_fusion.2), channel_id=1, source_target_pairs={{0,4},{2,6},{4,0},{6,2},{8,12},{10,14},{12,8},{14,10},{1,5},{3,7},... | collective-permute-start | bytes 294920 | tf_op jit(solution)/shard_map/ppermute | solution.py:29
  32.8 1.0 %collective-permute-done.5 = bf16[128,256]{1,0:T(8,128)(2,1)S(1)} collective-permute-done((bf16[128,256]{1,0:T(8,128)(2,1)S(1)}, bf16[128,256]{1,0:T(8,128)(2,1)S(1)}, u32[]{:S(2)}, u32[]{:S(2)}) %collective-permute-start.5) | collective-permute-done | bytes 65568 | tf_op jit(solution)/shard_map/ppermute | solution.py:29
  33.7 0.9 %collective-permute-start.6 = (bf16[128,256]{1,0:T(8,128)(2,1)S(1)}, bf16[128,256]{1,0:T(8,128)(2,1)S(1)}, u32[]{:S(2)}, u32[]{:S(2)}) collective-permute-start(bf16[128,256]{1,0:T(8,128)(2,1)S(1)} %add_convert_fusion.2), channel_id=1, source_target_pairs={{0,8},{2,10},{4,12},{6,14},{8,0},{10,2},{12,4},{14,6},{1,9},{3,11}... | collective-permute-start | bytes 196616 | tf_op jit(solution)/shard_map/ppermute | solution.py:29
  34.6 4.3 %collective-permute-done.6 = bf16[128,256]{1,0:T(8,128)(2,1)S(1)} collective-permute-done((bf16[128,256]{1,0:T(8,128)(2,1)S(1)}, bf16[128,256]{1,0:T(8,128)(2,1)S(1)}, u32[]{:S(2)}, u32[]{:S(2)}) %collective-permute-start.6) | collective-permute-done | bytes 65568 | tf_op jit(solution)/shard_map/ppermute | solution.py:29
  39.0 1.8 %collective-permute-start.7 = (bf16[128,256]{1,0:T(8,128)(2,1)S(1)}, bf16[128,256]{1,0:T(8,128)(2,1)S(1)}, u32[]{:S(2)}, u32[]{:S(2)}) collective-permute-start(bf16[128,256]{1,0:T(8,128)(2,1)S(1)} %add_convert_fusion.1), channel_id=1, source_target_pairs={{0,4},{2,6},{4,0},{6,2},{8,12},{10,14},{12,8},{14,10},{1,5},{3,7},... | collective-permute-start | bytes 196616 | tf_op jit(solution)/shard_map/ppermute | solution.py:29
  40.8 0.0 collective-permute-done.12
  40.8 1.1 %collective-permute-start.13 = (f32[384,128]{1,0:T(8,128)S(1)}, f32[384,128]{1,0:T(8,128)S(1)}, u32[]{:S(2)}, u32[]{:S(2)}) collective-permute-start(f32[384,128]{1,0:T(8,128)S(1)} %pad_maximum_fusion), channel_id=1, source_target_pairs={{0,2},{2,0},{4,6},{6,4},{8,10},{10,8},{12,14},{14,12},{1,3},{3,1},... | collective-permute-start | bytes 589832 | tf_op jit(solution)/shard_map/ppermute | solution.py:29
  41.9 1.4 %collective-permute-done.7 = bf16[128,256]{1,0:T(8,128)(2,1)S(1)} collective-permute-done((bf16[128,256]{1,0:T(8,128)(2,1)S(1)}, bf16[128,256]{1,0:T(8,128)(2,1)S(1)}, u32[]{:S(2)}, u32[]{:S(2)}) %collective-permute-start.7) | collective-permute-done | bytes 65568 | tf_op jit(solution)/shard_map/ppermute | solution.py:29
  43.4 0.8 %collective-permute-start.8 = (bf16[128,256]{1,0:T(8,128)(2,1)S(1)}, bf16[128,256]{1,0:T(8,128)(2,1)S(1)}, u32[]{:S(2)}, u32[]{:S(2)}) collective-permute-start(bf16[128,256]{1,0:T(8,128)(2,1)S(1)} %add_convert_fusion.a), channel_id=1, source_target_pairs={{0,2},{2,0},{4,6},{6,4},{8,10},{10,8},{12,14},{14,12},{1,3},{3,1},... | collective-permute-start | bytes 196616 | tf_op jit(solution)/shard_map/ppermute | solution.py:29
  44.2 3.5 %collective-permute-done.8.b = bf16[128,256]{1,0:T(8,128)(2,1)S(1)} collective-permute-done((bf16[128,256]{1,0:T(8,128)(2,1)S(1)}, bf16[128,256]{1,0:T(8,128)(2,1)S(1)}, u32[]{:S(2)}, u32[]{:S(2)}) %collective-permute-start.8) | collective-permute-done | bytes 65568 | tf_op jit(solution)/shard_map/ppermute | solution.py:29
  47.7 0.2 shard_map.132
  47.9 0.1 collective-permute-start.9
  47.9 0.0 collective-permute-done.13
  47.9 0.0 copy-start.2
  48.0 0.0 copy-start.3
  48.0 0.0 copy-start.4
  48.0 1.1 %collective-permute-done.9.sq_b = f32[8,128]{1,0:T(8,128)S(1)} collective-permute-done((f32[8,128]{1,0:T(8,128)S(1)}, f32[8,128]{1,0:T(8,128)S(1)}, u32[]{:S(2)}, u32[]{:S(2)}) %collective-permute-start.9) | collective-permute-done | bytes 4128 | tf_op jit(solution)/shard_map/ppermute | solution.py:29
  49.1 0.0 copy-done.2
  49.1 0.0 copy-done.3
  49.1 0.0 copy-done.4
  49.1 2.1 %shard_map.133 = (bf16[128,2048]{1,0:T(8,128)(2,1)}, f32[16,1,128]{2,1,0:T(1,128)}, f32[16,1,128]{2,1,0:T(1,128)}, f32[16,1,128]{2,1,0:T(1,128)}) custom-call(bf16[128,2048]{1,0:T(8,128)(2,1)S(1)} %bitcast.5, f32[2048,128]{1,0:T(8,128)S(1)} %get-tuple-element.23.acc_in, f32[2048,128]{1,0:T(8,128)S(1)} %get-tuple-element.24.total_in, ...), custom_call_target="tpu_custom_call" | custom-call | tf_op jit(solution)/shard_map/pallas_call | solution.py:320
  (12 shorter events, 0.1 us)
Async XLA Ops:
  0.6 23.3 %copy-start = (bf16[1,128,2048]{2,1,0:T(8,128)(2,1)S(1)}, bf16[1,128,2048]{2,1,0:T(8,128)(2,1)}, u32[]{:S(2)}) copy-start(bf16[1,128,2048]{2,1,0:T(8,128)(2,1)} %param.10) | copy-start | bytes 1572868
  1.6 8.2 %collective-permute-start = (bf16[304,128]{1,0:T(8,128)(2,1)S(1)}, bf16[304,128]{1,0:T(8,128)(2,1)S(1)}, u32[]{:S(2)}, u32[]{:S(2)}) collective-permute-start(bf16[304,128]{1,0:T(8,128)(2,1)S(1)} %get-tuple-element.19.refs_1_.refs_2_.refs_5_), channel_id=1, source_target_pairs={{0,8},{2,10},{4,12},{6,14},{8,0},{10,2},{12,4},{14,6},{1,9},{3,11}... | collective-permute-start | bytes 233480 | tf_op jit(solution)/shard_map/ppermute | solution.py:29
  9.8 5.3 %collective-permute-start.1 = (bf16[608,128]{1,0:T(8,128)(2,1)S(1)}, bf16[608,128]{1,0:T(8,128)(2,1)S(1)}, u32[]{:S(2)}, u32[]{:S(2)}) collective-permute-start(bf16[608,128]{1,0:T(8,128)(2,1)S(1)} %pad_maximum_fusion.1), channel_id=1, source_target_pairs={{0,4},{2,6},{4,0},{6,2},{8,12},{10,14},{12,8},{14,10},{1,5},{3,7},... | collective-permute-start | bytes 466952 | tf_op jit(solution)/shard_map/ppermute | solution.py:29
  10.6 9.5 %collective-permute-start.2 = (bf16[304,128]{1,0:T(8,128)(2,1)S(1)}, bf16[304,128]{1,0:T(8,128)(2,1)S(1)}, u32[]{:S(2)}, u32[]{:S(2)}) collective-permute-start(bf16[304,128]{1,0:T(8,128)(2,1)S(1)} %get-tuple-element.19.refs_1_.refs_2_.refs_5_), channel_id=1, source_target_pairs={{0,2},{2,0},{4,6},{6,4},{8,10},{10,8},{12,14},{14,12},{1,3},{3,1},... | collective-permute-start | bytes 233480 | tf_op jit(solution)/shard_map/ppermute | solution.py:29
  12.1 4.7 %collective-permute-start.10 = (f32[48,128]{1,0:T(8,128)S(1)}, f32[48,128]{1,0:T(8,128)S(1)}, u32[]{:S(2)}, u32[]{:S(2)}) collective-permute-start(f32[48,128]{1,0:T(8,128)S(1)} %get-tuple-element.29), channel_id=1, source_target_pairs={{0,16},{16,0},{1,17},{17,1},{2,18},{18,2},{3,19},{19,3},{4,20},{20... | collective-permute-start | bytes 73736 | tf_op jit(solution)/shard_map/ppermute | solution.py:29
  15.1 11.4 %collective-permute-start.4 = (bf16[608,128]{1,0:T(8,128)(2,1)S(1)}, bf16[608,128]{1,0:T(8,128)(2,1)S(1)}, u32[]{:S(2)}, u32[]{:S(2)}) collective-permute-start(bf16[608,128]{1,0:T(8,128)(2,1)S(1)} %collective-permute-done.1.refs_4_.refs_7_), channel_id=1, source_target_pairs={{0,2},{2,0},{4,6},{6,4},{8,10},{10,8},{12,14},{14,12},{1,3},{3,1},... | collective-permute-start | bytes 466952 | tf_op jit(solution)/shard_map/ppermute | solution.py:29
  16.8 14.1 %collective-permute-start.11 = (f32[96,128]{1,0:T(8,128)S(1)}, f32[96,128]{1,0:T(8,128)S(1)}, u32[]{:S(2)}, u32[]{:S(2)}) collective-permute-start(f32[96,128]{1,0:T(8,128)S(1)} %pad_maximum_fusion.3), channel_id=1, source_target_pairs={{0,8},{2,10},{4,12},{6,14},{8,0},{10,2},{12,4},{14,6},{1,9},{3,11}... | collective-permute-start | bytes 147464 | tf_op jit(solution)/shard_map/ppermute | solution.py:29
  19.5 4.4 %collective-permute-start.3 = (bf16[304,128]{1,0:T(8,128)(2,1)S(1)}, bf16[304,128]{1,0:T(8,128)(2,1)S(1)}, u32[]{:S(2)}, u32[]{:S(2)}) collective-permute-start(bf16[304,128]{1,0:T(8,128)(2,1)S(1)} %collective-permute-done.refs_3_.refs_6_), channel_id=1, source_target_pairs={{0,2},{2,0},{4,6},{6,4},{8,10},{10,8},{12,14},{14,12},{1,3},{3,1},... | collective-permute-start | bytes 233480 | tf_op jit(solution)/shard_map/ppermute | solution.py:29
  23.9 2.6 %copy-start.1 = (bf16[1,128,2048]{2,1,0:T(8,128)(2,1)S(1)}, bf16[1,128,2048]{2,1,0:T(8,128)(2,1)}, u32[]{:S(2)}) copy-start(bf16[1,128,2048]{2,1,0:T(8,128)(2,1)} %param.11) | copy-start | bytes 1572868
  29.4 4.3 %collective-permute-start.5 = (bf16[128,256]{1,0:T(8,128)(2,1)S(1)}, bf16[128,256]{1,0:T(8,128)(2,1)S(1)}, u32[]{:S(2)}, u32[]{:S(2)}) collective-permute-start(bf16[128,256]{1,0:T(8,128)(2,1)S(1)} %get-tuple-element.26), channel_id=1, source_target_pairs={{0,16},{16,0},{1,17},{17,1},{2,18},{18,2},{3,19},{19,3},{4,20},{20... | collective-permute-start | bytes 196616 | tf_op jit(solution)/shard_map/ppermute | solution.py:29
  31.0 9.8 %collective-permute-start.12 = (f32[192,128]{1,0:T(8,128)S(1)}, f32[192,128]{1,0:T(8,128)S(1)}, u32[]{:S(2)}, u32[]{:S(2)}) collective-permute-start(f32[192,128]{1,0:T(8,128)S(1)} %pad_maximum_fusion.2), channel_id=1, source_target_pairs={{0,4},{2,6},{4,0},{6,2},{8,12},{10,14},{12,8},{14,10},{1,5},{3,7},... | collective-permute-start | bytes 294920 | tf_op jit(solution)/shard_map/ppermute | solution.py:29
  33.7 5.3 %collective-permute-start.6 = (bf16[128,256]{1,0:T(8,128)(2,1)S(1)}, bf16[128,256]{1,0:T(8,128)(2,1)S(1)}, u32[]{:S(2)}, u32[]{:S(2)}) collective-permute-start(bf16[128,256]{1,0:T(8,128)(2,1)S(1)} %add_convert_fusion.2), channel_id=1, source_target_pairs={{0,8},{2,10},{4,12},{6,14},{8,0},{10,2},{12,4},{14,6},{1,9},{3,11}... | collective-permute-start | bytes 196616 | tf_op jit(solution)/shard_map/ppermute | solution.py:29
  39.0 4.3 %collective-permute-start.7 = (bf16[128,256]{1,0:T(8,128)(2,1)S(1)}, bf16[128,256]{1,0:T(8,128)(2,1)S(1)}, u32[]{:S(2)}, u32[]{:S(2)}) collective-permute-start(bf16[128,256]{1,0:T(8,128)(2,1)S(1)} %add_convert_fusion.1), channel_id=1, source_target_pairs={{0,4},{2,6},{4,0},{6,2},{8,12},{10,14},{12,8},{14,10},{1,5},{3,7},... | collective-permute-start | bytes 196616 | tf_op jit(solution)/shard_map/ppermute | solution.py:29
  40.8 7.1 %collective-permute-start.13 = (f32[384,128]{1,0:T(8,128)S(1)}, f32[384,128]{1,0:T(8,128)S(1)}, u32[]{:S(2)}, u32[]{:S(2)}) collective-permute-start(f32[384,128]{1,0:T(8,128)S(1)} %pad_maximum_fusion), channel_id=1, source_target_pairs={{0,2},{2,0},{4,6},{6,4},{8,10},{10,8},{12,14},{14,12},{1,3},{3,1},... | collective-permute-start | bytes 589832 | tf_op jit(solution)/shard_map/ppermute | solution.py:29
  43.4 4.3 %collective-permute-start.8 = (bf16[128,256]{1,0:T(8,128)(2,1)S(1)}, bf16[128,256]{1,0:T(8,128)(2,1)S(1)}, u32[]{:S(2)}, u32[]{:S(2)}) collective-permute-start(bf16[128,256]{1,0:T(8,128)(2,1)S(1)} %add_convert_fusion.a), channel_id=1, source_target_pairs={{0,2},{2,0},{4,6},{6,4},{8,10},{10,8},{12,14},{14,12},{1,3},{3,1},... | collective-permute-start | bytes 196616 | tf_op jit(solution)/shard_map/ppermute | solution.py:29
  47.9 1.2 %collective-permute-start.9 = (f32[8,128]{1,0:T(8,128)S(1)}, f32[8,128]{1,0:T(8,128)S(1)}, u32[]{:S(2)}, u32[]{:S(2)}) collective-permute-start(f32[8,128]{1,0:T(8,128)S(1)} %get-tuple-element.28.sq_a), channel_id=1, source_target_pairs={{0,1},{1,0},{2,3},{3,2},{4,5},{5,4},{6,7},{7,6},{8,9},{9,8},{10,11... | collective-permute-start | bytes 12296 | tf_op jit(solution)/shard_map/ppermute | solution.py:29
  47.9 1.1 %copy-start.2 = (f32[16,1,128]{2,1,0:T(1,128)S(1)}, f32[16,1,128]{2,1,0:T(1,128)}, u32[]{:S(2)}) copy-start(f32[16,1,128]{2,1,0:T(1,128)} %ma.3) | copy-start | bytes 24580
  48.0 1.1 %copy-start.3 = (f32[16,1,128]{2,1,0:T(1,128)S(1)}, f32[16,1,128]{2,1,0:T(1,128)}, u32[]{:S(2)}) copy-start(f32[16,1,128]{2,1,0:T(1,128)} %m1.3) | copy-start | bytes 24580
  48.0 1.1 %copy-start.4 = (f32[16,1,128]{2,1,0:T(1,128)S(1)}, f32[16,1,128]{2,1,0:T(1,128)}, u32[]{:S(2)}) copy-start(f32[16,1,128]{2,1,0:T(1,128)} %m2.3) | copy-start | bytes 24580
where the time goes:
time: 51.4 us; the launch traced here: 51.2 us
  starting transfers between devices  20.9 us (41%)
  waiting for transfers between devices  20.8 us (40%)
  Pallas kernels  8.63 us (17%)
  between operations  0.77 us (1%)
    ppermute x14, starting transfers between devices, swap(): return lax.ppermute(x, axis, [(i, i ^ mask) for i in range(size)])  20.9 us
    ppermute x14, waiting for transfers between devices, swap(): return lax.ppermute(x, axis, [(i, i ^ mask) for i in range(size)])  20.8 us
    pallas_call x1, Pallas kernels, local(): call(body, shapes + (sds((cart, 2 * hd), bf16),), 5 + len(msgs))  2.86 us
    pallas_call x1, Pallas kernels, local(): state = call(body, shapes, 1 + len(msgs))(q, msg, *msgs[:-1])  2.56 us
    pallas_call x1, Pallas kernels, local(): call(functools.partial(final_kernel, masks, dp_steps, scale, per, count),...  2.1 us
  transfers between devices with their start and end apart: 14, of which 8 were waited for; matrix products, arithmetic and copies ran while one was open for 0% of the time, Pallas kernels for 11%

commit v1 on v0

--- a/solution.py
+++ b/solution.py
@@ -29,11 +29,11 @@
     return lax.ppermute(x, axis, [(i, i ^ mask) for i in range(size)])
 
 
-def place(mask, steps):
+def spot(chain, axis, mask):
     at = 0
-    for n, step in enumerate(steps):
-        bit = step.bit_length() - 1
-        at = at + (((mask >> bit) & 1) << n)
+    for n, (name, step) in enumerate(chain):
+        if name == axis:
+            at = at + (((mask >> (step.bit_length() - 1)) & 1) << n)
     return at
 
 
@@ -186,8 +186,17 @@
         grad[pl.ds(to, crows)] = whole[j * crows : (j + 1) * crows]
 
 
-def square_kernel(a, b, total, squares):
-    g = a[...].astype(f32) + b[...].astype(f32)
+def summed(parts):
+    parts = [x.astype(f32) for x in parts]
+    if len(parts) == 2:
+        return parts[0] + parts[1]
+    own, one, two, both = parts
+    return (own + both) + (one + two)
+
+
+def square_kernel(*refs):
+    total, squares = refs[-2:]
+    g = summed([ref[...] for ref in refs[:-2]])
     total[...] = g
     squares[...] = jnp.broadcast_to(jnp.sum(g * g, keepdims=True), squares.shape)
 
@@ -198,10 +207,9 @@
     return one, two, ma - learn_rate * one / (jnp.sqrt(two) + adam_eps)
 
 
-def final_kernel(masks, dp_steps, scale, per, count, q, acc_in, total_in, top_in, g, sq_a, sq_b, st, ma, m1, m2, out, ma_o, m1_o, m2_o, cart):
+def final_kernel(masks, chain, n_dp, scale, per, count, q, acc_in, total_in, top_in, g, sq_a, sq_b, st, ma, m1, m2, out, ma_o, m1_o, m2_o, cart):
     rows, hd = q.shape[0], acc_in.shape[1]
     group = q.shape[1] // hd
-    n_dp = 1 << len(dp_steps)
     crows, width = ma.shape[0], ma.shape[2]
     me, my_dp = lax.axis_index("ctx"), lax.axis_index("dp")
     two = scale * log2_e
@@ -218,7 +226,7 @@
     for r, mask in enumerate(masks):
         parts = [[], [], []]
         for d in range(n_dp):
-            at = (r * n_dp + place(my_dp ^ d, dp_steps)) * 3 * crows
+            at = (spot(chain, "ctx", mask) + spot(chain, "dp", my_dp ^ d)) * 3 * crows
             for n in range(3):
                 parts[n].append(st[pl.ds(pl.multiple_of(at + n * crows, crows), crows)])
         ma_r, m1_r, m2_r = (jnp.concatenate(x, axis=1) for x in parts)
@@ -299,17 +307,21 @@
     msgs = pieces + mirrored
     body = functools.partial(chunk_kernel, len(msgs) - 1, scale, per, rows, stride)
     state = call(body, shapes, 1 + len(msgs))(q, msg, *msgs[:-1])
-    for axis, s, size in [("dp", s, n_dp) for s in dp_steps] + [("ctx", s, n_ctx) for s in steps]:
-        more = swap(st, axis, s, size)
+    chain = [("ctx", s) for s in steps]
+    chain[1:1] = [("dp", s) for s in dp_steps]
+    for axis, s in chain:
+        more = swap(st, axis, s, {"ctx": n_ctx, "dp": n_dp}[axis])
         st = jnp.concatenate([st, more], axis=0)
     body = functools.partial(gradient_kernel, 1, masks, scale, math.gcd(group, 8), rows, stride)
     *state, grad = call(body, shapes + (sds((cart, 2 * hd), bf16),), 5 + len(msgs))(q, t, *state, *msgs)
-    chain = [("dp", s, n_dp) for s in dp_steps] + [("ctx", s, n_ctx) for s in steps]
-    for n, (axis, s, size) in enumerate(chain):
-        other = swap(grad, axis, s, size)
-        if n + 1 < len(chain):
-            grad = (grad.astype(f32) + other.astype(f32)).astype(bf16)
-    total, squares = call(square_kernel, (sds((cart, 2 * hd), f32), sds((8, hd), f32)), 2)(grad, other)
+    bits = steps + [s * n_ctx for s in dp_steps]
+    rounds = [bits[n : n + 2] for n in range(0, len(bits), 2)]
+    for n, pair in enumerate(rounds):
+        ways = pair + [sum(pair)] if len(pair) == 2 else pair
+        others = [lax.ppermute(grad, ("dp", "ctx"), [(i, i ^ m) for i in range(n_dp * n_ctx)]) for m in ways]
+        if n + 1 < len(rounds):
+            grad = summed([grad] + others).astype(bf16)
+    total, squares = call(square_kernel, (sds((cart, 2 * hd), f32), sds((8, hd), f32)), 1 + len(others))(grad, *others)
     mine = squares
     theirs = jnp.zeros_like(squares)
     for n, s in enumerate(head_steps):
@@ -318,7 +330,7 @@
         theirs = swap(mine, "head", s, n_head)
     count = master.size * n_dp * n_ctx * n_head
     new_out, new_master, new_m1, new_m2 = call(
-        functools.partial(final_kernel, masks, dp_steps, scale, per, count),
+        functools.partial(final_kernel, masks, chain, n_dp, scale, per, count),
         (sds((rows, group * hd), bf16), sds(master.shape, f32), sds(master.shape, f32), sds(master.shape, f32)),
         11,
         [pltpu.VMEM((cart, 2 * hd), bf16)],

time: 51.4 us -> 48.9 us (0.951)
  waiting for transfers between devices: 20.8 us -> 17 us
  starting transfers between devices: 20.9 us -> 22.1 us
    ppermute x14 -> x10, waiting for transfers between devices: 20.8 us -> 9.79 us  [swap(): return lax.ppermute(x, axis, [(i, i ^ mask) for i in range(size)])]
    ppermute x0 -> x6, starting transfers between devices: none -> 8.01 us  [local(): lax.ppermute(grad, ('dp', 'ctx'), [(i, i ^ m) for i in range(n_dp * n_ctx)])]
    ppermute x0 -> x6, waiting for transfers between devices: none -> 7.24 us  [local(): lax.ppermute(grad, ('dp', 'ctx'), [(i, i ^ m) for i in range(n_dp * n_ctx)])]
    ppermute x14 -> x10, starting transfers between devices: 20.9 us -> 14.1 us  [swap(): return lax.ppermute(x, axis, [(i, i ^ mask) for i in range(size)])]
  transfers between devices with their start and end apart: 14 -> 16, of which waited for: 8 -> 10; matrix products, arithmetic and copies ran while one was open for 0% -> 0% of each run, Pallas kernels for 11% -> 12%
where the time goes in v1:
time: 48.9 us; the launch traced here: 48.7 us
  starting transfers between devices  22.1 us (45%)
  waiting for transfers between devices  17 us (35%)
  Pallas kernels  8.65 us (18%)
  between operations  0.77 us (2%)
    ppermute x10, starting transfers between devices, swap(): return lax.ppermute(x, axis, [(i, i ^ mask) for i in range(size)])  14.1 us
    ppermute x10, waiting for transfers between devices, swap(): return lax.ppermute(x, axis, [(i, i ^ mask) for i in range(size)])  9.79 us
    ppermute x6, starting transfers between devices, local(): lax.ppermute(grad, ('dp', 'ctx'), [(i, i ^ m) for i in range(n_dp * n_ctx)])  8.01 us
    ppermute x6, waiting for transfers between devices, local(): lax.ppermute(grad, ('dp', 'ctx'), [(i, i ^ m) for i in range(n_dp * n_ctx)])  7.24 us
    pallas_call x1, Pallas kernels, local(): call(body, shapes + (sds((cart, 2 * hd), bf16),), 5 + len(msgs))  2.86 us
    pallas_call x1, Pallas kernels, local(): state = call(body, shapes, 1 + len(msgs))(q, msg, *msgs[:-1])  2.56 us
    pallas_call x1, Pallas kernels, local(): call(functools.partial(final_kernel, masks, chain, n_dp, scale, per, coun...  2.09 us
  transfers between devices with their start and end apart: 16, of which 10 were waited for; matrix products, arithmetic and copies ran while one was open for 0% of the time, Pallas kernels for 12%

profile of v1, /device:TPU:0, one launch (start us, length us, event | category | flops | bytes accessed | tf_op | source)
XLA Modules:
  0.0 48.7 jit_solution(11942670610988880778)
XLA Ops:
  0.6 0.0 copy-start
  0.6 0.9 %shard_map.129 = (bf16[304,128]{1,0:T(8,128)(2,1)S(1)}, f32[48,128]{1,0:T(8,128)S(1)}) custom-call(bf16[1,128,128]{2,1,0:T(8,128)(2,1)} %k.1, bf16[1,128,128]{2,1,0:T(8,128)(2,1)} %v.1, s32[1,128]{1,0:T(1,128)} %pos.1, bf16[16,128]{1,0:T(8,128)(2,1)} %ck.1, bf16[16,128]{1,0:T(8,128)(2,1)} %cv.1, f32[16,1,128]{2,1,0:T(1,128)} %ma.3, f32[16,1,128]{2,1,0:T(1,128)} %m1.3, ...), custom_call_target="tpu_custom_call" | custom-call | tf_op jit(solution)/shard_map/pallas_call | solution.py:283
  1.6 4.1 %collective-permute-start = (bf16[304,128]{1,0:T(8,128)(2,1)S(1)}, bf16[304,128]{1,0:T(8,128)(2,1)S(1)}, u32[]{:S(2)}, u32[]{:S(2)}) collective-permute-start(bf16[304,128]{1,0:T(8,128)(2,1)S(1)} %get-tuple-element.19.refs_1_.refs_2_.refs_5_), channel_id=1, source_target_pairs={{0,8},{2,10},{4,12},{6,14},{8,0},{10,2},{12,4},{14,6},{1,9},{3,11}... | collective-permute-start | bytes 233480 | tf_op jit(solution)/shard_map/ppermute | solution.py:29
  5.7 1.5 %collective-permute-start.2 = (bf16[304,128]{1,0:T(8,128)(2,1)S(1)}, bf16[304,128]{1,0:T(8,128)(2,1)S(1)}, u32[]{:S(2)}, u32[]{:S(2)}) collective-permute-start(bf16[304,128]{1,0:T(8,128)(2,1)S(1)} %get-tuple-element.19.refs_1_.refs_2_.refs_5_), channel_id=1, source_target_pairs={{0,2},{2,0},{4,6},{6,4},{8,10},{10,8},{12,14},{14,12},{1,3},{3,1},... | collective-permute-start | bytes 233480 | tf_op jit(solution)/shard_map/ppermute | solution.py:29
  7.2 0.3 collective-permute-start.12
  7.6 2.2 %collective-permute-done.refs_3_.refs_6_ = bf16[304,128]{1,0:T(8,128)(2,1)S(1)} collective-permute-done((bf16[304,128]{1,0:T(8,128)(2,1)S(1)}, bf16[304,128]{1,0:T(8,128)(2,1)S(1)}, u32[]{:S(2)}, u32[]{:S(2)}) %collective-permute-start) | collective-permute-done | bytes 77856 | tf_op jit(solution)/shard_map/ppermute | solution.py:29
  9.8 1.6 %collective-permute-start.1 = (bf16[608,128]{1,0:T(8,128)(2,1)S(1)}, bf16[608,128]{1,0:T(8,128)(2,1)S(1)}, u32[]{:S(2)}, u32[]{:S(2)}) collective-permute-start(bf16[608,128]{1,0:T(8,128)(2,1)S(1)} %pad_maximum_fusion.1), channel_id=1, source_target_pairs={{0,4},{2,6},{4,0},{6,2},{8,12},{10,14},{12,8},{14,10},{1,5},{3,7},... | collective-permute-start | bytes 466952 | tf_op jit(solution)/shard_map/ppermute | solution.py:29
  11.4 0.7 %collective-permute-done.12 = f32[48,128]{1,0:T(8,128)S(1)} collective-permute-done((f32[48,128]{1,0:T(8,128)S(1)}, f32[48,128]{1,0:T(8,128)S(1)}, u32[]{:S(2)}, u32[]{:S(2)}) %collective-permute-start.12) | collective-permute-done | bytes 24608 | tf_op jit(solution)/shard_map/ppermute | solution.py:29
  12.1 1.5 %collective-permute-start.13 = (f32[96,128]{1,0:T(8,128)S(1)}, f32[96,128]{1,0:T(8,128)S(1)}, u32[]{:S(2)}, u32[]{:S(2)}) collective-permute-start(f32[96,128]{1,0:T(8,128)S(1)} %pad_maximum_fusion.3), channel_id=1, source_target_pairs={{0,16},{16,0},{1,17},{17,1},{2,18},{18,2},{3,19},{19,3},{4,20},{20... | collective-permute-start | bytes 147464 | tf_op jit(solution)/shard_map/ppermute | solution.py:29
  13.6 1.5 %collective-permute-done.1.refs_4_.refs_7_ = bf16[608,128]{1,0:T(8,128)(2,1)S(1)} collective-permute-done((bf16[608,128]{1,0:T(8,128)(2,1)S(1)}, bf16[608,128]{1,0:T(8,128)(2,1)S(1)}, u32[]{:S(2)}, u32[]{:S(2)}) %collective-permute-start.1) | collective-permute-done | bytes 155680 | tf_op jit(solution)/shard_map/ppermute | solution.py:29
  15.1 2.3 %collective-permute-start.4 = (bf16[608,128]{1,0:T(8,128)(2,1)S(1)}, bf16[608,128]{1,0:T(8,128)(2,1)S(1)}, u32[]{:S(2)}, u32[]{:S(2)}) collective-permute-start(bf16[608,128]{1,0:T(8,128)(2,1)S(1)} %collective-permute-done.1.refs_4_.refs_7_), channel_id=1, source_target_pairs={{0,2},{2,0},{4,6},{6,4},{8,10},{10,8},{12,14},{14,12},{1,3},{3,1},... | collective-permute-start | bytes 466952 | tf_op jit(solution)/shard_map/ppermute | solution.py:29
  17.3 0.0 collective-permute-done.13
  17.4 1.3 %collective-permute-start.14 = (f32[192,128]{1,0:T(8,128)S(1)}, f32[192,128]{1,0:T(8,128)S(1)}, u32[]{:S(2)}, u32[]{:S(2)}) collective-permute-start(f32[192,128]{1,0:T(8,128)S(1)} %pad_maximum_fusion.2), channel_id=1, source_target_pairs={{0,4},{2,6},{4,0},{6,2},{8,12},{10,14},{12,8},{14,10},{1,5},{3,7},... | collective-permute-start | bytes 294920 | tf_op jit(solution)/shard_map/ppermute | solution.py:29
  18.6 0.1 collective-permute-start.3
  18.7 0.0 collective-permute-done.2.refs_5_.refs_8_
  18.7 4.3 %collective-permute-done.3.refs_6_.refs_9_ = bf16[304,128]{1,0:T(8,128)(2,1)S(1)} collective-permute-done((bf16[304,128]{1,0:T(8,128)(2,1)S(1)}, bf16[304,128]{1,0:T(8,128)(2,1)S(1)}, u32[]{:S(2)}, u32[]{:S(2)}) %collective-permute-start.3) | collective-permute-done | bytes 77856 | tf_op jit(solution)/shard_map/ppermute | solution.py:29
  23.0 0.0 copy-done
  23.0 0.0 copy-start.1
  23.0 2.6 %shard_map.130 = (f32[2048,128]{1,0:T(8,128)S(1)}, f32[2048,128]{1,0:T(8,128)S(1)}, f32[2048,128]{1,0:T(8,128)S(1)}) custom-call(bf16[128,2048]{1,0:T(8,128)(2,1)S(1)} %bitcast.3, bf16[304,128]{1,0:T(8,128)(2,1)S(1)} %get-tuple-element.19.refs_1_.refs_2_.refs_5_, bf16[304,128]{1,0:T(8,128)(2,1)S(1)} %get-tuple-element.19.refs_1_.refs_2_.refs_5_, ...), custom_call_target="tpu_custom_call" | custom-call | tf_op jit(solution)/shard_map/pallas_call | solution.py:309
  25.6 0.0 collective-permute-done.4.refs_10_
  25.6 0.0 copy-done.1
  25.6 2.9 %shard_map.131 = (f32[2048,128]{1,0:T(8,128)S(1)}, f32[2048,128]{1,0:T(8,128)S(1)}, f32[2048,128]{1,0:T(8,128)S(1)}, bf16[128,256]{1,0:T(8,128)(2,1)S(1)}) custom-call(bf16[128,2048]{1,0:T(8,128)(2,1)S(1)} %bitcast.4, bf16[128,2048]{1,0:T(8,128)(2,1)S(1)} %bitcast.6, f32[2048,128]{1,0:T(8,128)S(1)} %get-tuple-element.20.refs_2_, ...), custom_call_target="tpu_custom_call" | custom-call | tf_op jit(solution)/shard_map/pallas_call | solution.py:316
  28.5 3.5 %collective-permute-start.5 = (bf16[128,256]{1,0:T(8,128)(2,1)S(1)}, bf16[128,256]{1,0:T(8,128)(2,1)S(1)}, u32[]{:S(2)}, u32[]{:S(2)}) collective-permute-start(bf16[128,256]{1,0:T(8,128)(2,1)S(1)} %get-tuple-element.26), channel_id=1, source_target_pairs={{0,12},{2,14},{4,8},{6,10},{8,4},{10,6},{12,0},{14,2},{16,28},{18,... | collective-permute-start | bytes 196616 | tf_op jit(solution)/shard_map/ppermute | solution.py:321
  32.0 0.0 collective-permute-start.6
  32.0 0.9 %collective-permute-start.7 = (bf16[128,256]{1,0:T(8,128)(2,1)S(1)}, bf16[128,256]{1,0:T(8,128)(2,1)S(1)}, u32[]{:S(2)}, u32[]{:S(2)}) collective-permute-start(bf16[128,256]{1,0:T(8,128)(2,1)S(1)} %get-tuple-element.26), channel_id=1, source_target_pairs={{0,4},{2,6},{4,0},{6,2},{8,12},{10,14},{12,8},{14,10},{16,20},{18,... | collective-permute-start | bytes 196616 | tf_op jit(solution)/shard_map/ppermute | solution.py:321
  32.9 0.0 collective-permute-done.14
  33.0 1.3 %collective-permute-start.15 = (f32[384,128]{1,0:T(8,128)S(1)}, f32[384,128]{1,0:T(8,128)S(1)}, u32[]{:S(2)}, u32[]{:S(2)}) collective-permute-start(f32[384,128]{1,0:T(8,128)S(1)} %pad_maximum_fusion), channel_id=1, source_target_pairs={{0,2},{2,0},{4,6},{6,4},{8,10},{10,8},{12,14},{14,12},{1,3},{3,1},... | collective-permute-start | bytes 589832 | tf_op jit(solution)/shard_map/ppermute | solution.py:29
  34.3 0.6 %collective-permute-done.5 = bf16[128,256]{1,0:T(8,128)(2,1)S(1)} collective-permute-done((bf16[128,256]{1,0:T(8,128)(2,1)S(1)}, bf16[128,256]{1,0:T(8,128)(2,1)S(1)}, u32[]{:S(2)}, u32[]{:S(2)}) %collective-permute-start.5) | collective-permute-done | bytes 65568 | tf_op jit(solution)/shard_map/ppermute | solution.py:321
  34.9 2.9 %collective-permute-done.6 = bf16[128,256]{1,0:T(8,128)(2,1)S(1)} collective-permute-done((bf16[128,256]{1,0:T(8,128)(2,1)S(1)}, bf16[128,256]{1,0:T(8,128)(2,1)S(1)}, u32[]{:S(2)}, u32[]{:S(2)}) %collective-permute-start.6) | collective-permute-done | bytes 65568 | tf_op jit(solution)/shard_map/ppermute | solution.py:321
  37.8 0.0 collective-permute-done.7
  37.8 1.9 %collective-permute-start.10 = (bf16[128,256]{1,0:T(8,128)(2,1)S(1)}, bf16[128,256]{1,0:T(8,128)(2,1)S(1)}, u32[]{:S(2)}, u32[]{:S(2)}) collective-permute-start(bf16[128,256]{1,0:T(8,128)(2,1)S(1)} %add_convert_fusion.refs_0_), channel_id=1, source_target_pairs={{0,18},{2,16},{4,22},{6,20},{8,26},{10,24},{12,30},{14,28},{16,2},... | collective-permute-start | bytes 196616 | tf_op jit(solution)/shard_map/ppermute | solution.py:321
  39.8 1.1 %collective-permute-start.8 = (bf16[128,256]{1,0:T(8,128)(2,1)S(1)}, bf16[128,256]{1,0:T(8,128)(2,1)S(1)}, u32[]{:S(2)}, u32[]{:S(2)}) collective-permute-start(bf16[128,256]{1,0:T(8,128)(2,1)S(1)} %add_convert_fusion.refs_0_), channel_id=1, source_target_pairs={{0,2},{2,0},{4,6},{6,4},{8,10},{10,8},{12,14},{14,12},{16,18},{18,... | collective-permute-start | bytes 196616 | tf_op jit(solution)/shard_map/ppermute | solution.py:321
  40.9 0.5 %collective-permute-start.9 = (bf16[128,256]{1,0:T(8,128)(2,1)S(1)}, bf16[128,256]{1,0:T(8,128)(2,1)S(1)}, u32[]{:S(2)}, u32[]{:S(2)}) collective-permute-start(bf16[128,256]{1,0:T(8,128)(2,1)S(1)} %add_convert_fusion.refs_0_), channel_id=1, source_target_pairs={{0,16},{2,18},{4,20},{6,22},{8,24},{10,26},{12,28},{14,30},{16,0},... | collective-permute-start | bytes 196616 | tf_op jit(solution)/shard_map/ppermute | solution.py:321
  41.4 1.7 %collective-permute-done.10.refs_3_ = bf16[128,256]{1,0:T(8,128)(2,1)S(1)} collective-permute-done((bf16[128,256]{1,0:T(8,128)(2,1)S(1)}, bf16[128,256]{1,0:T(8,128)(2,1)S(1)}, u32[]{:S(2)}, u32[]{:S(2)}) %collective-permute-start.10) | collective-permute-done | bytes 65568 | tf_op jit(solution)/shard_map/ppermute | solution.py:321
  43.1 1.0 %collective-permute-done.8.refs_1_ = bf16[128,256]{1,0:T(8,128)(2,1)S(1)} collective-permute-done((bf16[128,256]{1,0:T(8,128)(2,1)S(1)}, bf16[128,256]{1,0:T(8,128)(2,1)S(1)}, u32[]{:S(2)}, u32[]{:S(2)}) %collective-permute-start.8) | collective-permute-done | bytes 65568 | tf_op jit(solution)/shard_map/ppermute | solution.py:321
  44.0 1.1 %collective-permute-done.9.refs_2_ = bf16[128,256]{1,0:T(8,128)(2,1)S(1)} collective-permute-done((bf16[128,256]{1,0:T(8,128)(2,1)S(1)}, bf16[128,256]{1,0:T(8,128)(2,1)S(1)}, u32[]{:S(2)}, u32[]{:S(2)}) %collective-permute-start.9) | collective-permute-done | bytes 65568 | tf_op jit(solution)/shard_map/ppermute | solution.py:321
  45.1 0.2 shard_map.132
  45.3 0.1 collective-permute-start.11
  45.4 0.0 collective-permute-done.15
  45.4 0.0 copy-start.2
  45.4 0.0 copy-start.3
  45.4 0.0 copy-start.4
  45.5 1.1 %collective-permute-done.11.sq_b = f32[8,128]{1,0:T(8,128)S(1)} collective-permute-done((f32[8,128]{1,0:T(8,128)S(1)}, f32[8,128]{1,0:T(8,128)S(1)}, u32[]{:S(2)}, u32[]{:S(2)}) %collective-permute-start.11) | collective-permute-done | bytes 4128 | tf_op jit(solution)/shard_map/ppermute | solution.py:29
  46.6 0.0 copy-done.2
  46.6 0.0 copy-done.3
  46.6 0.0 copy-done.4
  46.6 2.1 %shard_map.133 = (bf16[128,2048]{1,0:T(8,128)(2,1)}, f32[16,1,128]{2,1,0:T(1,128)}, f32[16,1,128]{2,1,0:T(1,128)}, f32[16,1,128]{2,1,0:T(1,128)}) custom-call(bf16[128,2048]{1,0:T(8,128)(2,1)S(1)} %bitcast.5, f32[2048,128]{1,0:T(8,128)S(1)} %get-tuple-element.23.acc_in, f32[2048,128]{1,0:T(8,128)S(1)} %get-tuple-element.24.total_in, ...), custom_call_target="tpu_custom_call" | custom-call | tf_op jit(solution)/shard_map/pallas_call | solution.py:332
  (10 shorter events, 0.1 us)
Async XLA Ops:
  0.6 22.4 %copy-start = (bf16[1,128,2048]{2,1,0:T(8,128)(2,1)S(1)}, bf16[1,128,2048]{2,1,0:T(8,128)(2,1)}, u32[]{:S(2)}) copy-start(bf16[1,128,2048]{2,1,0:T(8,128)(2,1)} %param.10) | copy-start | bytes 1572868
  1.6 8.2 %collective-permute-start = (bf16[304,128]{1,0:T(8,128)(2,1)S(1)}, bf16[304,128]{1,0:T(8,128)(2,1)S(1)}, u32[]{:S(2)}, u32[]{:S(2)}) collective-permute-start(bf16[304,128]{1,0:T(8,128)(2,1)S(1)} %get-tuple-element.19.refs_1_.refs_2_.refs_5_), channel_id=1, source_target_pairs={{0,8},{2,10},{4,12},{6,14},{8,0},{10,2},{12,4},{14,6},{1,9},{3,11}... | collective-permute-start | bytes 233480 | tf_op jit(solution)/shard_map/ppermute | solution.py:29
  5.7 13.0 %collective-permute-start.2 = (bf16[304,128]{1,0:T(8,128)(2,1)S(1)}, bf16[304,128]{1,0:T(8,128)(2,1)S(1)}, u32[]{:S(2)}, u32[]{:S(2)}) collective-permute-start(bf16[304,128]{1,0:T(8,128)(2,1)S(1)} %get-tuple-element.19.refs_1_.refs_2_.refs_5_), channel_id=1, source_target_pairs={{0,2},{2,0},{4,6},{6,4},{8,10},{10,8},{12,14},{14,12},{1,3},{3,1},... | collective-permute-start | bytes 233480 | tf_op jit(solution)/shard_map/ppermute | solution.py:29
  7.2 4.8 %collective-permute-start.12 = (f32[48,128]{1,0:T(8,128)S(1)}, f32[48,128]{1,0:T(8,128)S(1)}, u32[]{:S(2)}, u32[]{:S(2)}) collective-permute-start(f32[48,128]{1,0:T(8,128)S(1)} %get-tuple-element.29), channel_id=1, source_target_pairs={{0,8},{2,10},{4,12},{6,14},{8,0},{10,2},{12,4},{14,6},{1,9},{3,11}... | collective-permute-start | bytes 73736 | tf_op jit(solution)/shard_map/ppermute | solution.py:29
  9.8 5.3 %collective-permute-start.1 = (bf16[608,128]{1,0:T(8,128)(2,1)S(1)}, bf16[608,128]{1,0:T(8,128)(2,1)S(1)}, u32[]{:S(2)}, u32[]{:S(2)}) collective-permute-start(bf16[608,128]{1,0:T(8,128)(2,1)S(1)} %pad_maximum_fusion.1), channel_id=1, source_target_pairs={{0,4},{2,6},{4,0},{6,2},{8,12},{10,14},{12,8},{14,10},{1,5},{3,7},... | collective-permute-start | bytes 466952 | tf_op jit(solution)/shard_map/ppermute | solution.py:29
  12.1 5.3 %collective-permute-start.13 = (f32[96,128]{1,0:T(8,128)S(1)}, f32[96,128]{1,0:T(8,128)S(1)}, u32[]{:S(2)}, u32[]{:S(2)}) collective-permute-start(f32[96,128]{1,0:T(8,128)S(1)} %pad_maximum_fusion.3), channel_id=1, source_target_pairs={{0,16},{16,0},{1,17},{17,1},{2,18},{18,2},{3,19},{19,3},{4,20},{20... | collective-permute-start | bytes 147464 | tf_op jit(solution)/shard_map/ppermute | solution.py:29
  15.1 10.5 %collective-permute-start.4 = (bf16[608,128]{1,0:T(8,128)(2,1)S(1)}, bf16[608,128]{1,0:T(8,128)(2,1)S(1)}, u32[]{:S(2)}, u32[]{:S(2)}) collective-permute-start(bf16[608,128]{1,0:T(8,128)(2,1)S(1)} %collective-permute-done.1.refs_4_.refs_7_), channel_id=1, source_target_pairs={{0,2},{2,0},{4,6},{6,4},{8,10},{10,8},{12,14},{14,12},{1,3},{3,1},... | collective-permute-start | bytes 466952 | tf_op jit(solution)/shard_map/ppermute | solution.py:29
  17.4 15.6 %collective-permute-start.14 = (f32[192,128]{1,0:T(8,128)S(1)}, f32[192,128]{1,0:T(8,128)S(1)}, u32[]{:S(2)}, u32[]{:S(2)}) collective-permute-start(f32[192,128]{1,0:T(8,128)S(1)} %pad_maximum_fusion.2), channel_id=1, source_target_pairs={{0,4},{2,6},{4,0},{6,2},{8,12},{10,14},{12,8},{14,10},{1,5},{3,7},... | collective-permute-start | bytes 294920 | tf_op jit(solution)/shard_map/ppermute | solution.py:29
  18.6 4.4 %collective-permute-start.3 = (bf16[304,128]{1,0:T(8,128)(2,1)S(1)}, bf16[304,128]{1,0:T(8,128)(2,1)S(1)}, u32[]{:S(2)}, u32[]{:S(2)}) collective-permute-start(bf16[304,128]{1,0:T(8,128)(2,1)S(1)} %collective-permute-done.refs_3_.refs_6_), channel_id=1, source_target_pairs={{0,2},{2,0},{4,6},{6,4},{8,10},{10,8},{12,14},{14,12},{1,3},{3,1},... | collective-permute-start | bytes 233480 | tf_op jit(solution)/shard_map/ppermute | solution.py:29
  23.0 2.6 %copy-start.1 = (bf16[1,128,2048]{2,1,0:T(8,128)(2,1)S(1)}, bf16[1,128,2048]{2,1,0:T(8,128)(2,1)}, u32[]{:S(2)}) copy-start(bf16[1,128,2048]{2,1,0:T(8,128)(2,1)} %param.11) | copy-start | bytes 1572868
  28.5 6.4 %collective-permute-start.5 = (bf16[128,256]{1,0:T(8,128)(2,1)S(1)}, bf16[128,256]{1,0:T(8,128)(2,1)S(1)}, u32[]{:S(2)}, u32[]{:S(2)}) collective-permute-start(bf16[128,256]{1,0:T(8,128)(2,1)S(1)} %get-tuple-element.26), channel_id=1, source_target_pairs={{0,12},{2,14},{4,8},{6,10},{8,4},{10,6},{12,0},{14,2},{16,28},{18,... | collective-permute-start | bytes 196616 | tf_op jit(solution)/shard_map/ppermute | solution.py:321
  32.0 5.8 %collective-permute-start.6 = (bf16[128,256]{1,0:T(8,128)(2,1)S(1)}, bf16[128,256]{1,0:T(8,128)(2,1)S(1)}, u32[]{:S(2)}, u32[]{:S(2)}) collective-permute-start(bf16[128,256]{1,0:T(8,128)(2,1)S(1)} %get-tuple-element.26), channel_id=1, source_target_pairs={{0,8},{2,10},{4,12},{6,14},{8,0},{10,2},{12,4},{14,6},{16,24},{18,... | collective-permute-start | bytes 196616 | tf_op jit(solution)/shard_map/ppermute | solution.py:321
  32.0 5.8 %collective-permute-start.7 = (bf16[128,256]{1,0:T(8,128)(2,1)S(1)}, bf16[128,256]{1,0:T(8,128)(2,1)S(1)}, u32[]{:S(2)}, u32[]{:S(2)}) collective-permute-start(bf16[128,256]{1,0:T(8,128)(2,1)S(1)} %get-tuple-element.26), channel_id=1, source_target_pairs={{0,4},{2,6},{4,0},{6,2},{8,12},{10,14},{12,8},{14,10},{16,20},{18,... | collective-permute-start | bytes 196616 | tf_op jit(solution)/shard_map/ppermute | solution.py:321
  33.0 12.4 %collective-permute-start.15 = (f32[384,128]{1,0:T(8,128)S(1)}, f32[384,128]{1,0:T(8,128)S(1)}, u32[]{:S(2)}, u32[]{:S(2)}) collective-permute-start(f32[384,128]{1,0:T(8,128)S(1)} %pad_maximum_fusion), channel_id=1, source_target_pairs={{0,2},{2,0},{4,6},{6,4},{8,10},{10,8},{12,14},{14,12},{1,3},{3,1},... | collective-permute-start | bytes 589832 | tf_op jit(solution)/shard_map/ppermute | solution.py:29
  37.8 5.2 %collective-permute-start.10 = (bf16[128,256]{1,0:T(8,128)(2,1)S(1)}, bf16[128,256]{1,0:T(8,128)(2,1)S(1)}, u32[]{:S(2)}, u32[]{:S(2)}) collective-permute-start(bf16[128,256]{1,0:T(8,128)(2,1)S(1)} %add_convert_fusion.refs_0_), channel_id=1, source_target_pairs={{0,18},{2,16},{4,22},{6,20},{8,26},{10,24},{12,30},{14,28},{16,2},... | collective-permute-start | bytes 196616 | tf_op jit(solution)/shard_map/ppermute | solution.py:321
  39.8 4.3 %collective-permute-start.8 = (bf16[128,256]{1,0:T(8,128)(2,1)S(1)}, bf16[128,256]{1,0:T(8,128)(2,1)S(1)}, u32[]{:S(2)}, u32[]{:S(2)}) collective-permute-start(bf16[128,256]{1,0:T(8,128)(2,1)S(1)} %add_convert_fusion.refs_0_), channel_id=1, source_target_pairs={{0,2},{2,0},{4,6},{6,4},{8,10},{10,8},{12,14},{14,12},{16,18},{18,... | collective-permute-start | bytes 196616 | tf_op jit(solution)/shard_map/ppermute | solution.py:321
  40.9 4.3 %collective-permute-start.9 = (bf16[128,256]{1,0:T(8,128)(2,1)S(1)}, bf16[128,256]{1,0:T(8,128)(2,1)S(1)}, u32[]{:S(2)}, u32[]{:S(2)}) collective-permute-start(bf16[128,256]{1,0:T(8,128)(2,1)S(1)} %add_convert_fusion.refs_0_), channel_id=1, source_target_pairs={{0,16},{2,18},{4,20},{6,22},{8,24},{10,26},{12,28},{14,30},{16,0},... | collective-permute-start | bytes 196616 | tf_op jit(solution)/shard_map/ppermute | solution.py:321
  45.3 1.2 %collective-permute-start.11 = (f32[8,128]{1,0:T(8,128)S(1)}, f32[8,128]{1,0:T(8,128)S(1)}, u32[]{:S(2)}, u32[]{:S(2)}) collective-permute-start(f32[8,128]{1,0:T(8,128)S(1)} %get-tuple-element.28.sq_a), channel_id=1, source_target_pairs={{0,1},{1,0},{2,3},{3,2},{4,5},{5,4},{6,7},{7,6},{8,9},{9,8},{10,11... | collective-permute-start | bytes 12296 | tf_op jit(solution)/shard_map/ppermute | solution.py:29
  45.4 1.1 %copy-start.2 = (f32[16,1,128]{2,1,0:T(1,128)S(1)}, f32[16,1,128]{2,1,0:T(1,128)}, u32[]{:S(2)}) copy-start(f32[16,1,128]{2,1,0:T(1,128)} %ma.3) | copy-start | bytes 24580
  45.4 1.1 %copy-start.3 = (f32[16,1,128]{2,1,0:T(1,128)S(1)}, f32[16,1,128]{2,1,0:T(1,128)}, u32[]{:S(2)}) copy-start(f32[16,1,128]{2,1,0:T(1,128)} %m1.3) | copy-start | bytes 24580
  45.4 1.1 %copy-start.4 = (f32[16,1,128]{2,1,0:T(1,128)S(1)}, f32[16,1,128]{2,1,0:T(1,128)}, u32[]{:S(2)}) copy-start(f32[16,1,128]{2,1,0:T(1,128)} %m2.3) | copy-start | bytes 24580

commit v2 on v1

--- a/solution.py
+++ b/solution.py
@@ -27,6 +27,10 @@
 
 def swap(x, axis, mask, size):
     return lax.ppermute(x, axis, [(i, i ^ mask) for i in range(size)])
+
+
+def joined(parts):
+    return jnp.concatenate(parts, axis=0) if len(parts) > 1 else parts[0]
 
 
 def spot(chain, axis, mask):
@@ -207,7 +211,7 @@
     return one, two, ma - learn_rate * one / (jnp.sqrt(two) + adam_eps)
 
 
-def final_kernel(masks, chain, n_dp, scale, per, count, q, acc_in, total_in, top_in, g, sq_a, sq_b, st, ma, m1, m2, out, ma_o, m1_o, m2_o, cart):
+def final_kernel(masks, chain, n_dp, scale, per, count, q, acc_in, total_in, top_in, g, sq_a, sq_b, st_near, st_far, ma, m1, m2, out, ma_o, m1_o, m2_o, cart):
     rows, hd = q.shape[0], acc_in.shape[1]
     group = q.shape[1] // hd
     crows, width = ma.shape[0], ma.shape[2]
@@ -225,8 +229,9 @@
     ma_o[:, 0, :] = new
     for r, mask in enumerate(masks):
         parts = [[], [], []]
+        st = st_far if mask & chain[-1][1] else st_near
         for d in range(n_dp):
-            at = (spot(chain, "ctx", mask) + spot(chain, "dp", my_dp ^ d)) * 3 * crows
+            at = (spot(chain[:-1], "ctx", mask) + spot(chain[:-1], "dp", my_dp ^ d)) * 3 * crows
             for n in range(3):
                 parts[n].append(st[pl.ds(pl.multiple_of(at + n * crows, crows), crows)])
         ma_r, m1_r, m2_r = (jnp.concatenate(x, axis=1) for x in parts)
@@ -297,28 +302,30 @@
     cart = n_ctx * crows
     shapes = (sds((rows * group, hd), f32),) * 3
     last = steps[-1]
-    pieces, mirrored, held = [msg], [], msg
+    held, fresh, mirrored = [msg], [msg], []
     for s in steps[:-1]:
-        piece = swap(held, "ctx", s, n_ctx)
-        mirrored.append(swap(pieces[-1], "ctx", last, n_ctx))
-        held = jnp.concatenate([held, piece], axis=0)
-        pieces.append(piece)
-    mirrored.append(swap(pieces[-1], "ctx", last, n_ctx))
-    msgs = pieces + mirrored
+        older = held[: len(held) - len(fresh)]
+        got = [swap(joined(older), "ctx", s, n_ctx)] if older else []
+        got.append(swap(joined(fresh), "ctx", s, n_ctx))
+        mirrored.append(swap(joined(fresh), "ctx", last, n_ctx))
+        held, fresh = held + got, got
+    mirrored.append(swap(joined(fresh), "ctx", last, n_ctx))
+    msgs = held + mirrored
     body = functools.partial(chunk_kernel, len(msgs) - 1, scale, per, rows, stride)
     state = call(body, shapes, 1 + len(msgs))(q, msg, *msgs[:-1])
     chain = [("ctx", s) for s in steps]
     chain[1:1] = [("dp", s) for s in dp_steps]
-    for axis, s in chain:
+    for n, (axis, s) in enumerate(chain):
+        if n:
+            st = lax.optimization_barrier(jnp.concatenate([st, more], axis=0))
         more = swap(st, axis, s, {"ctx": n_ctx, "dp": n_dp}[axis])
-        st = jnp.concatenate([st, more], axis=0)
     body = functools.partial(gradient_kernel, 1, masks, scale, math.gcd(group, 8), rows, stride)
     *state, grad = call(body, shapes + (sds((cart, 2 * hd), bf16),), 5 + len(msgs))(q, t, *state, *msgs)
     bits = steps + [s * n_ctx for s in dp_steps]
     rounds = [bits[n : n + 2] for n in range(0, len(bits), 2)]
     for n, pair in enumerate(rounds):
         ways = pair + [sum(pair)] if len(pair) == 2 else pair
-        others = [lax.ppermute(grad, ("dp", "ctx"), [(i, i ^ m) for i in range(n_dp * n_ctx)]) for m in ways]
+        others = [swap(grad, ("dp", "ctx"), m, n_dp * n_ctx) for m in ways]
         if n + 1 < len(rounds):
             grad = summed([grad] + others).astype(bf16)
     total, squares = call(square_kernel, (sds((cart, 2 * hd), f32), sds((8, hd), f32)), 1 + len(others))(grad, *others)
@@ -332,9 +339,9 @@
     new_out, new_master, new_m1, new_m2 = call(
         functools.partial(final_kernel, masks, chain, n_dp, scale, per, count),
         (sds((rows, group * hd), bf16), sds(master.shape, f32), sds(master.shape, f32), sds(master.shape, f32)),
-        11,
+        12,
         [pltpu.VMEM((cart, 2 * hd), bf16)],
-    )(q, *state, total, mine, theirs, st, master, first_moment1, second_moment2)
+    )(q, *state, total, mine, theirs, st, more, master, first_moment1, second_moment2)
     return (new_out[None], new_master, new_m1, new_m2)
 
 

time: 48.9 us -> 48.5 us (level)
  waiting for transfers between devices: 17 us -> 16.4 us
    ppermute x10 -> x17, starting transfers between devices: 14.1 us -> 22.4 us  [swap(): return lax.ppermute(x, axis, [(i, i ^ mask) for i in range(size)])]
    ppermute x6 -> x0, starting transfers between devices: 8.01 us -> none  [local(): lax.ppermute(grad, ('dp', 'ctx'), [(i, i ^ m) for i in range(n_dp * n_ctx)])]
    ppermute x6 -> x0, waiting for transfers between devices: 7.24 us -> none  [local(): lax.ppermute(grad, ('dp', 'ctx'), [(i, i ^ m) for i in range(n_dp * n_ctx)])]
    ppermute x10 -> x17, waiting for transfers between devices: 9.79 us -> 16.4 us  [swap(): return lax.ppermute(x, axis, [(i, i ^ mask) for i in range(size)])]
  transfers between devices with their start and end apart: 16 -> 17, of which waited for: 10 -> 10; matrix products, arithmetic and copies ran while one was open for 0% -> 0% of each run, Pallas kernels for 12% -> 12%
where the time goes in v2:
time: 48.5 us; the launch traced here: 48.3 us
  starting transfers between devices  22.4 us (46%)
  waiting for transfers between devices  16.4 us (34%)
  Pallas kernels  8.7 us (18%)
  between operations  0.74 us (2%)
    ppermute x17, starting transfers between devices, swap(): return lax.ppermute(x, axis, [(i, i ^ mask) for i in range(size)])  22.4 us
    ppermute x17, waiting for transfers between devices, swap(): return lax.ppermute(x, axis, [(i, i ^ mask) for i in range(size)])  16.4 us
    pallas_call x1, Pallas kernels, local(): call(body, shapes + (sds((cart, 2 * hd), bf16),), 5 + len(msgs))  2.9 us
    pallas_call x1, Pallas kernels, local(): state = call(body, shapes, 1 + len(msgs))(q, msg, *msgs[:-1])  2.56 us
    pallas_call x1, Pallas kernels, local(): call(functools.partial(final_kernel, masks, chain, n_dp, scale, per, coun...  2.09 us
  transfers between devices with their start and end apart: 17, of which 10 were waited for; matrix products, arithmetic and copies ran while one was open for 0% of the time, Pallas kernels for 12%

profile of v2, /device:TPU:0, one launch (start us, length us, event | category | flops | bytes accessed | tf_op | source)
XLA Modules:
  0.0 48.3 jit_solution(4971247319603723438)
XLA Ops:
  0.6 0.0 copy-start
  0.6 0.9 %shard_map.129 = (bf16[304,128]{1,0:T(8,128)(2,1)S(1)}, f32[48,128]{1,0:T(8,128)S(1)}) custom-call(bf16[1,128,128]{2,1,0:T(8,128)(2,1)} %k.1, bf16[1,128,128]{2,1,0:T(8,128)(2,1)} %v.1, s32[1,128]{1,0:T(1,128)} %pos.1, bf16[16,128]{1,0:T(8,128)(2,1)} %ck.1, bf16[16,128]{1,0:T(8,128)(2,1)} %cv.1, f32[16,1,128]{2,1,0:T(1,128)} %ma.3, f32[16,1,128]{2,1,0:T(1,128)} %m1.3, ...), custom_call_target="tpu_custom_call" | custom-call | tf_op jit(solution)/shard_map/pallas_call | solution.py:288
  1.6 4.1 %collective-permute-start = (bf16[304,128]{1,0:T(8,128)(2,1)S(1)}, bf16[304,128]{1,0:T(8,128)(2,1)S(1)}, u32[]{:S(2)}, u32[]{:S(2)}) collective-permute-start(bf16[304,128]{1,0:T(8,128)(2,1)S(1)} %get-tuple-element.19.refs_1_.refs_2_.refs_5_), channel_id=1, source_target_pairs={{0,8},{2,10},{4,12},{6,14},{8,0},{10,2},{12,4},{14,6},{1,9},{3,11}... | collective-permute-start | bytes 233480 | tf_op jit(solution)/shard_map/ppermute | solution.py:29
  5.7 0.1 collective-permute-start.13
  5.8 1.8 %collective-permute-start.1 = (bf16[304,128]{1,0:T(8,128)(2,1)S(1)}, bf16[304,128]{1,0:T(8,128)(2,1)S(1)}, u32[]{:S(2)}, u32[]{:S(2)}) collective-permute-start(bf16[304,128]{1,0:T(8,128)(2,1)S(1)} %get-tuple-element.19.refs_1_.refs_2_.refs_5_), channel_id=1, source_target_pairs={{0,4},{2,6},{4,0},{6,2},{8,12},{10,14},{12,8},{14,10},{1,5},{3,7},... | collective-permute-start | bytes 233480 | tf_op jit(solution)/shard_map/ppermute | solution.py:29
  7.6 2.7 %collective-permute-done.refs_3_.refs_6_ = bf16[304,128]{1,0:T(8,128)(2,1)S(1)} collective-permute-done((bf16[304,128]{1,0:T(8,128)(2,1)S(1)}, bf16[304,128]{1,0:T(8,128)(2,1)S(1)}, u32[]{:S(2)}, u32[]{:S(2)}) %collective-permute-start) | collective-permute-done | bytes 77856 | tf_op jit(solution)/shard_map/ppermute | solution.py:29
  10.3 0.8 %collective-permute-start.2 = (bf16[304,128]{1,0:T(8,128)(2,1)S(1)}, bf16[304,128]{1,0:T(8,128)(2,1)S(1)}, u32[]{:S(2)}, u32[]{:S(2)}) collective-permute-start(bf16[304,128]{1,0:T(8,128)(2,1)S(1)} %collective-permute-done.refs_3_.refs_6_), channel_id=1, source_target_pairs={{0,4},{2,6},{4,0},{6,2},{8,12},{10,14},{12,8},{14,10},{1,5},{3,7},... | collective-permute-start | bytes 233480 | tf_op jit(solution)/shard_map/ppermute | solution.py:29
  11.1 0.0 collective-permute-done.13
  11.1 1.6 %collective-permute-start.14 = (f32[96,128]{1,0:T(8,128)S(1)}, f32[96,128]{1,0:T(8,128)S(1)}, u32[]{:S(2)}, u32[]{:S(2)}) collective-permute-start(f32[96,128]{1,0:T(8,128)S(1)} %pad_maximum_fusion.3), channel_id=1, source_target_pairs={{0,16},{16,0},{1,17},{17,1},{2,18},{18,2},{3,19},{19,3},{4,20},{20... | collective-permute-start | bytes 147464 | tf_op jit(solution)/shard_map/ppermute | solution.py:29
  12.7 0.0 collective-permute-done.1.refs_4_.refs_7_
  12.7 2.0 %collective-permute-done.2.refs_5_.refs_8_ = bf16[304,128]{1,0:T(8,128)(2,1)S(1)} collective-permute-done((bf16[304,128]{1,0:T(8,128)(2,1)S(1)}, bf16[304,128]{1,0:T(8,128)(2,1)S(1)}, u32[]{:S(2)}, u32[]{:S(2)}) %collective-permute-start.2) | collective-permute-done | bytes 77856 | tf_op jit(solution)/shard_map/ppermute | solution.py:29
  14.7 1.8 %collective-permute-start.5 = (bf16[608,128]{1,0:T(8,128)(2,1)S(1)}, bf16[608,128]{1,0:T(8,128)(2,1)S(1)}, u32[]{:S(2)}, u32[]{:S(2)}) collective-permute-start(bf16[608,128]{1,0:T(8,128)(2,1)S(1)} %pad_maximum_fusion.1), channel_id=1, source_target_pairs={{0,2},{2,0},{4,6},{6,4},{8,10},{10,8},{12,14},{14,12},{1,3},{3,1},... | collective-permute-start | bytes 466952 | tf_op jit(solution)/shard_map/ppermute | solution.py:29
  16.5 0.0 collective-permute-done.14
  16.5 0.7 %collective-permute-start.15 = (f32[192,128]{1,0:T(8,128)S(1)}, f32[192,128]{1,0:T(8,128)S(1)}, u32[]{:S(2)}, u32[]{:S(2)}) collective-permute-start(f32[192,128]{1,0:T(8,128)S(1)} %pad_maximum_fusion.2), channel_id=1, source_target_pairs={{0,4},{2,6},{4,0},{6,2},{8,12},{10,14},{12,8},{14,10},{1,5},{3,7},... | collective-permute-start | bytes 294920 | tf_op jit(solution)/shard_map/ppermute | solution.py:29
  17.2 1.1 %collective-permute-start.3 = (bf16[304,128]{1,0:T(8,128)(2,1)S(1)}, bf16[304,128]{1,0:T(8,128)(2,1)S(1)}, u32[]{:S(2)}, u32[]{:S(2)}) collective-permute-start(bf16[304,128]{1,0:T(8,128)(2,1)S(1)} %get-tuple-element.19.refs_1_.refs_2_.refs_5_), channel_id=1, source_target_pairs={{0,2},{2,0},{4,6},{6,4},{8,10},{10,8},{12,14},{14,12},{1,3},{3,1},... | collective-permute-start | bytes 233480 | tf_op jit(solution)/shard_map/ppermute | solution.py:29
  18.3 0.9 %collective-permute-start.4 = (bf16[304,128]{1,0:T(8,128)(2,1)S(1)}, bf16[304,128]{1,0:T(8,128)(2,1)S(1)}, u32[]{:S(2)}, u32[]{:S(2)}) collective-permute-start(bf16[304,128]{1,0:T(8,128)(2,1)S(1)} %collective-permute-done.refs_3_.refs_6_), channel_id=1, source_target_pairs={{0,2},{2,0},{4,6},{6,4},{8,10},{10,8},{12,14},{14,12},{1,3},{3,1},... | collective-permute-start | bytes 233480 | tf_op jit(solution)/shard_map/ppermute | solution.py:29
  19.2 2.8 %collective-permute-done.3.refs_6_.refs_9_ = bf16[304,128]{1,0:T(8,128)(2,1)S(1)} collective-permute-done((bf16[304,128]{1,0:T(8,128)(2,1)S(1)}, bf16[304,128]{1,0:T(8,128)(2,1)S(1)}, u32[]{:S(2)}, u32[]{:S(2)}) %collective-permute-start.3) | collective-permute-done | bytes 77856 | tf_op jit(solution)/shard_map/ppermute | solution.py:29
  22.0 0.8 %collective-permute-done.4.refs_7_.refs_10_ = bf16[304,128]{1,0:T(8,128)(2,1)S(1)} collective-permute-done((bf16[304,128]{1,0:T(8,128)(2,1)S(1)}, bf16[304,128]{1,0:T(8,128)(2,1)S(1)}, u32[]{:S(2)}, u32[]{:S(2)}) %collective-permute-start.4) | collective-permute-done | bytes 77856 | tf_op jit(solution)/shard_map/ppermute | solution.py:29
  22.8 0.0 copy-done
  22.8 0.0 copy-start.1
  22.8 2.6 %shard_map.130 = (f32[2048,128]{1,0:T(8,128)S(1)}, f32[2048,128]{1,0:T(8,128)S(1)}, f32[2048,128]{1,0:T(8,128)S(1)}) custom-call(bf16[128,2048]{1,0:T(8,128)(2,1)S(1)} %bitcast.3, bf16[304,128]{1,0:T(8,128)(2,1)S(1)} %get-tuple-element.19.refs_1_.refs_2_.refs_5_, bf16[304,128]{1,0:T(8,128)(2,1)S(1)} %get-tuple-element.19.refs_1_.refs_2_.refs_5_, ...), custom_call_target="tpu_custom_call" | custom-call | tf_op jit(solution)/shard_map/pallas_call | solution.py:315
  25.4 0.0 collective-permute-done.5.refs_11_
  25.4 0.0 copy-done.1
  25.4 2.9 %shard_map.131 = (f32[2048,128]{1,0:T(8,128)S(1)}, f32[2048,128]{1,0:T(8,128)S(1)}, f32[2048,128]{1,0:T(8,128)S(1)}, bf16[128,256]{1,0:T(8,128)(2,1)S(1)}) custom-call(bf16[128,2048]{1,0:T(8,128)(2,1)S(1)} %bitcast.4, bf16[128,2048]{1,0:T(8,128)(2,1)S(1)} %bitcast.6, f32[2048,128]{1,0:T(8,128)S(1)} %get-tuple-element.20.refs_2_, ...), custom_call_target="tpu_custom_call" | custom-call | tf_op jit(solution)/shard_map/pallas_call | solution.py:323
  28.3 3.7 %collective-permute-start.6 = (bf16[128,256]{1,0:T(8,128)(2,1)S(1)}, bf16[128,256]{1,0:T(8,128)(2,1)S(1)}, u32[]{:S(2)}, u32[]{:S(2)}) collective-permute-start(bf16[128,256]{1,0:T(8,128)(2,1)S(1)} %get-tuple-element.26), channel_id=1, source_target_pairs={{0,12},{2,14},{4,8},{6,10},{8,4},{10,6},{12,0},{14,2},{16,28},{18,... | collective-permute-start | bytes 196616 | tf_op jit(solution)/shard_map/ppermute | solution.py:29
  32.0 0.0 collective-permute-start.7
  32.0 0.8 %collective-permute-start.8 = (bf16[128,256]{1,0:T(8,128)(2,1)S(1)}, bf16[128,256]{1,0:T(8,128)(2,1)S(1)}, u32[]{:S(2)}, u32[]{:S(2)}) collective-permute-start(bf16[128,256]{1,0:T(8,128)(2,1)S(1)} %get-tuple-element.26), channel_id=1, source_target_pairs={{0,4},{2,6},{4,0},{6,2},{8,12},{10,14},{12,8},{14,10},{16,20},{18,... | collective-permute-start | bytes 196616 | tf_op jit(solution)/shard_map/ppermute | solution.py:29
  32.8 0.0 collective-permute-done.15
  32.8 1.4 %collective-permute-start.16 = (f32[384,128]{1,0:T(8,128)S(1)}, f32[384,128]{1,0:T(8,128)S(1)}, u32[]{:S(2)}, u32[]{:S(2)}) collective-permute-start(f32[384,128]{1,0:T(8,128)S(1)} %pad_maximum_fusion.st_near), channel_id=1, source_target_pairs={{0,2},{2,0},{4,6},{6,4},{8,10},{10,8},{12,14},{14,12},{1,3},{3,1},... | collective-permute-start | bytes 589832 | tf_op jit(solution)/shard_map/ppermute | solution.py:29
  34.2 0.5 %collective-permute-done.6 = bf16[128,256]{1,0:T(8,128)(2,1)S(1)} collective-permute-done((bf16[128,256]{1,0:T(8,128)(2,1)S(1)}, bf16[128,256]{1,0:T(8,128)(2,1)S(1)}, u32[]{:S(2)}, u32[]{:S(2)}) %collective-permute-start.6) | collective-permute-done | bytes 65568 | tf_op jit(solution)/shard_map/ppermute | solution.py:29
  34.7 2.6 %collective-permute-done.7 = bf16[128,256]{1,0:T(8,128)(2,1)S(1)} collective-permute-done((bf16[128,256]{1,0:T(8,128)(2,1)S(1)}, bf16[128,256]{1,0:T(8,128)(2,1)S(1)}, u32[]{:S(2)}, u32[]{:S(2)}) %collective-permute-start.7) | collective-permute-done | bytes 65568 | tf_op jit(solution)/shard_map/ppermute | solution.py:29
  37.3 0.0 collective-permute-done.8
  37.4 1.6 %collective-permute-start.10 = (bf16[128,256]{1,0:T(8,128)(2,1)S(1)}, bf16[128,256]{1,0:T(8,128)(2,1)S(1)}, u32[]{:S(2)}, u32[]{:S(2)}) collective-permute-start(bf16[128,256]{1,0:T(8,128)(2,1)S(1)} %add_convert_fusion.refs_0_), channel_id=1, source_target_pairs={{0,16},{2,18},{4,20},{6,22},{8,24},{10,26},{12,28},{14,30},{16,0},... | collective-permute-start | bytes 196616 | tf_op jit(solution)/shard_map/ppermute | solution.py:29
  38.9 1.3 %collective-permute-start.11 = (bf16[128,256]{1,0:T(8,128)(2,1)S(1)}, bf16[128,256]{1,0:T(8,128)(2,1)S(1)}, u32[]{:S(2)}, u32[]{:S(2)}) collective-permute-start(bf16[128,256]{1,0:T(8,128)(2,1)S(1)} %add_convert_fusion.refs_0_), channel_id=1, source_target_pairs={{0,18},{2,16},{4,22},{6,20},{8,26},{10,24},{12,30},{14,28},{16,2},... | collective-permute-start | bytes 196616 | tf_op jit(solution)/shard_map/ppermute | solution.py:29
  40.2 0.7 %collective-permute-start.9 = (bf16[128,256]{1,0:T(8,128)(2,1)S(1)}, bf16[128,256]{1,0:T(8,128)(2,1)S(1)}, u32[]{:S(2)}, u32[]{:S(2)}) collective-permute-start(bf16[128,256]{1,0:T(8,128)(2,1)S(1)} %add_convert_fusion.refs_0_), channel_id=1, source_target_pairs={{0,2},{2,0},{4,6},{6,4},{8,10},{10,8},{12,14},{14,12},{16,18},{18,... | collective-permute-start | bytes 196616 | tf_op jit(solution)/shard_map/ppermute | solution.py:29
  40.9 0.8 %collective-permute-done.10.refs_2_ = bf16[128,256]{1,0:T(8,128)(2,1)S(1)} collective-permute-done((bf16[128,256]{1,0:T(8,128)(2,1)S(1)}, bf16[128,256]{1,0:T(8,128)(2,1)S(1)}, u32[]{:S(2)}, u32[]{:S(2)}) %collective-permute-start.10) | collective-permute-done | bytes 65568 | tf_op jit(solution)/shard_map/ppermute | solution.py:29
  41.7 2.4 %collective-permute-done.11.refs_3_ = bf16[128,256]{1,0:T(8,128)(2,1)S(1)} collective-permute-done((bf16[128,256]{1,0:T(8,128)(2,1)S(1)}, bf16[128,256]{1,0:T(8,128)(2,1)S(1)}, u32[]{:S(2)}, u32[]{:S(2)}) %collective-permute-start.11) | collective-permute-done | bytes 65568 | tf_op jit(solution)/shard_map/ppermute | solution.py:29
  44.1 0.7 %collective-permute-done.9.refs_1_ = bf16[128,256]{1,0:T(8,128)(2,1)S(1)} collective-permute-done((bf16[128,256]{1,0:T(8,128)(2,1)S(1)}, bf16[128,256]{1,0:T(8,128)(2,1)S(1)}, u32[]{:S(2)}, u32[]{:S(2)}) %collective-permute-start.9) | collective-permute-done | bytes 65568 | tf_op jit(solution)/shard_map/ppermute | solution.py:29
  44.8 0.0 copy-start.3
  44.8 0.2 shard_map.132
  45.0 0.0 copy-start.2
  45.0 0.1 collective-permute-start.12
  45.1 0.0 collective-permute-done.16.st_far
  45.1 1.1 %collective-permute-done.12.sq_b = f32[8,128]{1,0:T(8,128)S(1)} collective-permute-done((f32[8,128]{1,0:T(8,128)S(1)}, f32[8,128]{1,0:T(8,128)S(1)}, u32[]{:S(2)}, u32[]{:S(2)}) %collective-permute-start.12) | collective-permute-done | bytes 4128 | tf_op jit(solution)/shard_map/ppermute | solution.py:29
  46.2 0.0 copy-done.3
  46.2 0.0 copy-done.4
  46.2 0.0 copy-done.2
  46.2 2.1 %shard_map.133 = (bf16[128,2048]{1,0:T(8,128)(2,1)}, f32[16,1,128]{2,1,0:T(1,128)}, f32[16,1,128]{2,1,0:T(1,128)}, f32[16,1,128]{2,1,0:T(1,128)}) custom-call(bf16[128,2048]{1,0:T(8,128)(2,1)S(1)} %bitcast.5, f32[2048,128]{1,0:T(8,128)S(1)} %get-tuple-element.23.acc_in, f32[2048,128]{1,0:T(8,128)S(1)} %get-tuple-element.24.total_in, ...), custom_call_target="tpu_custom_call" | custom-call | tf_op jit(solution)/shard_map/pallas_call | solution.py:339
  (6 shorter events, 0.1 us)
Async XLA Ops:
  0.6 22.2 %copy-start = (bf16[1,128,2048]{2,1,0:T(8,128)(2,1)S(1)}, bf16[1,128,2048]{2,1,0:T(8,128)(2,1)}, u32[]{:S(2)}) copy-start(bf16[1,128,2048]{2,1,0:T(8,128)(2,1)} %param.10) | copy-start | bytes 1572868
  1.6 8.7 %collective-permute-start = (bf16[304,128]{1,0:T(8,128)(2,1)S(1)}, bf16[304,128]{1,0:T(8,128)(2,1)S(1)}, u32[]{:S(2)}, u32[]{:S(2)}) collective-permute-start(bf16[304,128]{1,0:T(8,128)(2,1)S(1)} %get-tuple-element.19.refs_1_.refs_2_.refs_5_), channel_id=1, source_target_pairs={{0,8},{2,10},{4,12},{6,14},{8,0},{10,2},{12,4},{14,6},{1,9},{3,11}... | collective-permute-start | bytes 233480 | tf_op jit(solution)/shard_map/ppermute | solution.py:29
  5.7 5.4 %collective-permute-start.13 = (f32[48,128]{1,0:T(8,128)S(1)}, f32[48,128]{1,0:T(8,128)S(1)}, u32[]{:S(2)}, u32[]{:S(2)}) collective-permute-start(f32[48,128]{1,0:T(8,128)S(1)} %get-tuple-element.29), channel_id=1, source_target_pairs={{0,8},{2,10},{4,12},{6,14},{8,0},{10,2},{12,4},{14,6},{1,9},{3,11}... | collective-permute-start | bytes 73736 | tf_op jit(solution)/shard_map/ppermute | solution.py:29
  5.8 6.8 %collective-permute-start.1 = (bf16[304,128]{1,0:T(8,128)(2,1)S(1)}, bf16[304,128]{1,0:T(8,128)(2,1)S(1)}, u32[]{:S(2)}, u32[]{:S(2)}) collective-permute-start(bf16[304,128]{1,0:T(8,128)(2,1)S(1)} %get-tuple-element.19.refs_1_.refs_2_.refs_5_), channel_id=1, source_target_pairs={{0,4},{2,6},{4,0},{6,2},{8,12},{10,14},{12,8},{14,10},{1,5},{3,7},... | collective-permute-start | bytes 233480 | tf_op jit(solution)/shard_map/ppermute | solution.py:29
  10.3 4.4 %collective-permute-start.2 = (bf16[304,128]{1,0:T(8,128)(2,1)S(1)}, bf16[304,128]{1,0:T(8,128)(2,1)S(1)}, u32[]{:S(2)}, u32[]{:S(2)}) collective-permute-start(bf16[304,128]{1,0:T(8,128)(2,1)S(1)} %collective-permute-done.refs_3_.refs_6_), channel_id=1, source_target_pairs={{0,4},{2,6},{4,0},{6,2},{8,12},{10,14},{12,8},{14,10},{1,5},{3,7},... | collective-permute-start | bytes 233480 | tf_op jit(solution)/shard_map/ppermute | solution.py:29
  11.1 5.4 %collective-permute-start.14 = (f32[96,128]{1,0:T(8,128)S(1)}, f32[96,128]{1,0:T(8,128)S(1)}, u32[]{:S(2)}, u32[]{:S(2)}) collective-permute-start(f32[96,128]{1,0:T(8,128)S(1)} %pad_maximum_fusion.3), channel_id=1, source_target_pairs={{0,16},{16,0},{1,17},{17,1},{2,18},{18,2},{3,19},{19,3},{4,20},{20... | collective-permute-start | bytes 147464 | tf_op jit(solution)/shard_map/ppermute | solution.py:29
  14.7 10.7 %collective-permute-start.5 = (bf16[608,128]{1,0:T(8,128)(2,1)S(1)}, bf16[608,128]{1,0:T(8,128)(2,1)S(1)}, u32[]{:S(2)}, u32[]{:S(2)}) collective-permute-start(bf16[608,128]{1,0:T(8,128)(2,1)S(1)} %pad_maximum_fusion.1), channel_id=1, source_target_pairs={{0,2},{2,0},{4,6},{6,4},{8,10},{10,8},{12,14},{14,12},{1,3},{3,1},... | collective-permute-start | bytes 466952 | tf_op jit(solution)/shard_map/ppermute | solution.py:29
  16.5 16.3 %collective-permute-start.15 = (f32[192,128]{1,0:T(8,128)S(1)}, f32[192,128]{1,0:T(8,128)S(1)}, u32[]{:S(2)}, u32[]{:S(2)}) collective-permute-start(f32[192,128]{1,0:T(8,128)S(1)} %pad_maximum_fusion.2), channel_id=1, source_target_pairs={{0,4},{2,6},{4,0},{6,2},{8,12},{10,14},{12,8},{14,10},{1,5},{3,7},... | collective-permute-start | bytes 294920 | tf_op jit(solution)/shard_map/ppermute | solution.py:29
  17.2 4.8 %collective-permute-start.3 = (bf16[304,128]{1,0:T(8,128)(2,1)S(1)}, bf16[304,128]{1,0:T(8,128)(2,1)S(1)}, u32[]{:S(2)}, u32[]{:S(2)}) collective-permute-start(bf16[304,128]{1,0:T(8,128)(2,1)S(1)} %get-tuple-element.19.refs_1_.refs_2_.refs_5_), channel_id=1, source_target_pairs={{0,2},{2,0},{4,6},{6,4},{8,10},{10,8},{12,14},{14,12},{1,3},{3,1},... | collective-permute-start | bytes 233480 | tf_op jit(solution)/shard_map/ppermute | solution.py:29
  18.3 4.6 %collective-permute-start.4 = (bf16[304,128]{1,0:T(8,128)(2,1)S(1)}, bf16[304,128]{1,0:T(8,128)(2,1)S(1)}, u32[]{:S(2)}, u32[]{:S(2)}) collective-permute-start(bf16[304,128]{1,0:T(8,128)(2,1)S(1)} %collective-permute-done.refs_3_.refs_6_), channel_id=1, source_target_pairs={{0,2},{2,0},{4,6},{6,4},{8,10},{10,8},{12,14},{14,12},{1,3},{3,1},... | collective-permute-start | bytes 233480 | tf_op jit(solution)/shard_map/ppermute | solution.py:29
  22.8 2.6 %copy-start.1 = (bf16[1,128,2048]{2,1,0:T(8,128)(2,1)S(1)}, bf16[1,128,2048]{2,1,0:T(8,128)(2,1)}, u32[]{:S(2)}) copy-start(bf16[1,128,2048]{2,1,0:T(8,128)(2,1)} %param.11) | copy-start | bytes 1572868
  28.3 6.4 %collective-permute-start.6 = (bf16[128,256]{1,0:T(8,128)(2,1)S(1)}, bf16[128,256]{1,0:T(8,128)(2,1)S(1)}, u32[]{:S(2)}, u32[]{:S(2)}) collective-permute-start(bf16[128,256]{1,0:T(8,128)(2,1)S(1)} %get-tuple-element.26), channel_id=1, source_target_pairs={{0,12},{2,14},{4,8},{6,10},{8,4},{10,6},{12,0},{14,2},{16,28},{18,... | collective-permute-start | bytes 196616 | tf_op jit(solution)/shard_map/ppermute | solution.py:29
  32.0 5.3 %collective-permute-start.7 = (bf16[128,256]{1,0:T(8,128)(2,1)S(1)}, bf16[128,256]{1,0:T(8,128)(2,1)S(1)}, u32[]{:S(2)}, u32[]{:S(2)}) collective-permute-start(bf16[128,256]{1,0:T(8,128)(2,1)S(1)} %get-tuple-element.26), channel_id=1, source_target_pairs={{0,8},{2,10},{4,12},{6,14},{8,0},{10,2},{12,4},{14,6},{16,24},{18,... | collective-permute-start | bytes 196616 | tf_op jit(solution)/shard_map/ppermute | solution.py:29
  32.0 5.3 %collective-permute-start.8 = (bf16[128,256]{1,0:T(8,128)(2,1)S(1)}, bf16[128,256]{1,0:T(8,128)(2,1)S(1)}, u32[]{:S(2)}, u32[]{:S(2)}) collective-permute-start(bf16[128,256]{1,0:T(8,128)(2,1)S(1)} %get-tuple-element.26), channel_id=1, source_target_pairs={{0,4},{2,6},{4,0},{6,2},{8,12},{10,14},{12,8},{14,10},{16,20},{18,... | collective-permute-start | bytes 196616 | tf_op jit(solution)/shard_map/ppermute | solution.py:29
  32.8 12.3 %collective-permute-start.16 = (f32[384,128]{1,0:T(8,128)S(1)}, f32[384,128]{1,0:T(8,128)S(1)}, u32[]{:S(2)}, u32[]{:S(2)}) collective-permute-start(f32[384,128]{1,0:T(8,128)S(1)} %pad_maximum_fusion.st_near), channel_id=1, source_target_pairs={{0,2},{2,0},{4,6},{6,4},{8,10},{10,8},{12,14},{14,12},{1,3},{3,1},... | collective-permute-start | bytes 589832 | tf_op jit(solution)/shard_map/ppermute | solution.py:29
  37.4 4.3 %collective-permute-start.10 = (bf16[128,256]{1,0:T(8,128)(2,1)S(1)}, bf16[128,256]{1,0:T(8,128)(2,1)S(1)}, u32[]{:S(2)}, u32[]{:S(2)}) collective-permute-start(bf16[128,256]{1,0:T(8,128)(2,1)S(1)} %add_convert_fusion.refs_0_), channel_id=1, source_target_pairs={{0,16},{2,18},{4,20},{6,22},{8,24},{10,26},{12,28},{14,30},{16,0},... | collective-permute-start | bytes 196616 | tf_op jit(solution)/shard_map/ppermute | solution.py:29
  38.9 5.2 %collective-permute-start.11 = (bf16[128,256]{1,0:T(8,128)(2,1)S(1)}, bf16[128,256]{1,0:T(8,128)(2,1)S(1)}, u32[]{:S(2)}, u32[]{:S(2)}) collective-permute-start(bf16[128,256]{1,0:T(8,128)(2,1)S(1)} %add_convert_fusion.refs_0_), channel_id=1, source_target_pairs={{0,18},{2,16},{4,22},{6,20},{8,26},{10,24},{12,30},{14,28},{16,2},... | collective-permute-start | bytes 196616 | tf_op jit(solution)/shard_map/ppermute | solution.py:29
  40.2 4.5 %collective-permute-start.9 = (bf16[128,256]{1,0:T(8,128)(2,1)S(1)}, bf16[128,256]{1,0:T(8,128)(2,1)S(1)}, u32[]{:S(2)}, u32[]{:S(2)}) collective-permute-start(bf16[128,256]{1,0:T(8,128)(2,1)S(1)} %add_convert_fusion.refs_0_), channel_id=1, source_target_pairs={{0,2},{2,0},{4,6},{6,4},{8,10},{10,8},{12,14},{14,12},{16,18},{18,... | collective-permute-start | bytes 196616 | tf_op jit(solution)/shard_map/ppermute | solution.py:29
  44.8 1.4 %copy-start.3 = (f32[16,1,128]{2,1,0:T(1,128)S(1)}, f32[16,1,128]{2,1,0:T(1,128)}, u32[]{:S(2)}) copy-start(f32[16,1,128]{2,1,0:T(1,128)} %m1.3) | copy-start | bytes 24580
  44.8 1.4 %copy-start.4 = (f32[16,1,128]{2,1,0:T(1,128)S(1)}, f32[16,1,128]{2,1,0:T(1,128)}, u32[]{:S(2)}) copy-start(f32[16,1,128]{2,1,0:T(1,128)} %m2.3) | copy-start | bytes 24580
  45.0 1.3 %copy-start.2 = (f32[16,1,128]{2,1,0:T(1,128)S(1)}, f32[16,1,128]{2,1,0:T(1,128)}, u32[]{:S(2)}) copy-start(f32[16,1,128]{2,1,0:T(1,128)} %ma.3) | copy-start | bytes 24580
  45.0 1.2 %collective-permute-start.12 = (f32[8,128]{1,0:T(8,128)S(1)}, f32[8,128]{1,0:T(8,128)S(1)}, u32[]{:S(2)}, u32[]{:S(2)}) collective-permute-start(f32[8,128]{1,0:T(8,128)S(1)} %get-tuple-element.28.sq_a), channel_id=1, source_target_pairs={{0,1},{1,0},{2,3},{3,2},{4,5},{5,4},{6,7},{7,6},{8,9},{9,8},{10,11... | collective-permute-start | bytes 12296 | tf_op jit(solution)/shard_map/ppermute | solution.py:29
